TPU v7x, 256 devices: a whole 4x4x8 slice. The times are simulated.
256 devices in a mesh: scene: 8 (over x, core), region: 32 (over z, y).
Axes of the slice: x: 4, y: 4, z: 8, core: 2. Of those that a mesh axis runs over, the one named last changes fastest.
Arguments:
- tiles: bfloat16 [8, 64, 32, 32, 256], P('scene', 'region'), may hold values from -6 to 6
- cotangent: bfloat16 [8, 64, 16, 16, 256], P('scene', 'region'), may hold values from -6 to 6
- positions: int32 [8, 64], P('scene', 'region'), may hold values from 0 to 63, each once within a row
- clear: int32 [8, 64], P('scene', 'region'), may hold values 0 or 1
- w_first: bfloat16 [2304, 256], P('scene'), may hold values from -0.125 to 0.125
- w_second: bfloat16 [2304, 256], P('scene'), may hold values from -0.125 to 0.125
Outputs:
- features: bfloat16 [8, 64, 16, 16, 256], P('scene', 'region')
- grad_first: float32 [2304, 256], P('region', 'scene')
- grad_second: float32 [2304, 256], P('region', 'scene')
Inputs may be any that keep to these rules, and one draw needn't show every extreme that they name: Each scene's row is a permutation of the grid positions 0 to 63.
All inputs are finite; a program needn't handle non-finite values. No bound on the sum of `clear` on one device may be relied on, other than what follows from the above.
Results may differ from a plain program's by a relative error of at most 0.005.
Values may be sent and summed in bfloat16 or wider, within the bound.
A program may use at most 128 MiB of HBM per device.

v0:
```python
import math

import jax
import jax.numpy as jnp
from jax import lax
from jax.sharding import PartitionSpec as P

GW = 4


def silu_slope(pre_act):
    sigmoid_v = jax.nn.sigmoid(pre_act)
    return sigmoid_v * (1.0 + pre_act * (1.0 - sigmoid_v))


def tap_patches(padded, out_side, stride):
    windows = []
    for tap_row in range(3):
        for tap_col in range(3):
            windows.append(
                padded[
                    :,
                    tap_row : tap_row + stride * out_side : stride,
                    tap_col : tap_col + stride * out_side : stride,
                    :,
                ]
            )
    stacked = jnp.concatenate(windows, axis=-1)
    return stacked.reshape(-1, stacked.shape[-1])


def shift_down(values, axis_num):
    widths = [(0, 0)] * values.ndim
    widths[axis_num] = (1, 0)
    padded = jnp.pad(values, widths)
    return lax.slice_in_dim(padded, 0, values.shape[axis_num], 1, axis_num)


def local(tiles, cotangent, positions, clear, w_first, w_second):
    tiles_here = tiles[0]
    slot_count = tiles_here.shape[0]
    tile_side = tiles_here.shape[1]
    tile_half = tile_side // 2
    channels = tiles_here.shape[3]
    local_pos = positions[0]
    every_pos = lax.all_gather(positions, "region", axis=1, tiled=True)[0]
    tile_count = every_pos.shape[0]
    grid_rows = tile_count // GW
    slot_ids = jnp.arange(tile_count, dtype=jnp.int32)
    onehot = (every_pos[:, None] == slot_ids[None, :]).astype(jnp.int32)
    slot_of = jnp.sum(onehot * slot_ids[:, None], axis=0)
    row_here = local_pos // GW
    col_here = local_pos % GW

    def fetch(all_rims, down, sideways, which):
        new_row = row_here + down
        new_col = col_here + sideways
        inside = (new_row >= 0) & (new_row < grid_rows) & (new_col >= 0) & (new_col < GW)
        position = jnp.clip(new_row, 0, grid_rows - 1) * GW + jnp.clip(new_col, 0, GW - 1)
        picked = jnp.take(all_rims, jnp.take(slot_of, position), axis=0)[:, which]
        return picked * inside.astype(picked.dtype)[:, None, None]

    edge_rims = jnp.stack(
        [
            tiles_here[:, 0],
            tiles_here[:, tile_side - 1],
            tiles_here[:, :, 0],
            tiles_here[:, :, tile_side - 1],
        ],
        axis=1,
    )
    all_edges = lax.all_gather(edge_rims, "region", axis=0, tiled=True)
    above_row = fetch(all_edges, -1, 0, 1)
    below_row = fetch(all_edges, 1, 0, 0)
    left_col = fetch(all_edges, 0, -1, 3)
    right_col = fetch(all_edges, 0, 1, 2)
    corner_ul = fetch(all_edges, -1, -1, 1)[:, tile_side - 1]
    corner_ur = fetch(all_edges, -1, 1, 1)[:, 0]
    corner_dl = fetch(all_edges, 1, -1, 0)[:, tile_side - 1]
    corner_dr = fetch(all_edges, 1, 1, 0)[:, 0]
    upper = jnp.concatenate([corner_ul[:, None], above_row, corner_ur[:, None]], axis=1)
    lower = jnp.concatenate([corner_dl[:, None], below_row, corner_dr[:, None]], axis=1)
    middle = jnp.concatenate([left_col[:, :, None], tiles_here, right_col[:, :, None]], axis=2)
    input_pad = jnp.concatenate([upper[:, None], middle, lower[:, None]], axis=1)
    patches_first = tap_patches(input_pad, tile_side, 1)
    pre_flat = jnp.dot(
        patches_first,
        lax.all_gather(w_first, "scene", axis=0, tiled=True),
        preferred_element_type=jnp.float32,
    )
    second_full = lax.all_gather(w_second, "scene", axis=0, tiled=True)
    pre_act = pre_flat.reshape(slot_count, tile_side, tile_side, channels)
    hidden = jax.nn.silu(pre_act).astype(jnp.bfloat16)
    hidden_rims = jnp.stack([hidden[:, tile_side - 1], hidden[:, :, tile_side - 1]], axis=1)
    all_hidden = lax.all_gather(hidden_rims, "region", axis=0, tiled=True)
    hidden_above = fetch(all_hidden, -1, 0, 0)
    hidden_left = fetch(all_hidden, 0, -1, 1)
    hidden_corner = fetch(all_hidden, -1, -1, 0)[:, tile_side - 1]
    hidden_top = jnp.concatenate([hidden_corner[:, None], hidden_above], axis=1)
    hidden_body = jnp.concatenate([hidden_left[:, :, None], hidden], axis=2)
    hidden_pad = jnp.concatenate([hidden_top[:, None], hidden_body], axis=1)
    patches_second = tap_patches(hidden_pad, tile_half, 2)
    out_flat = jnp.dot(patches_second, second_full, preferred_element_type=jnp.float32)
    features = out_flat.astype(jnp.bfloat16).reshape(1, slot_count, tile_half, tile_half, channels)
    masked = cotangent[0] * clear[0].astype(jnp.bfloat16)[:, None, None, None]
    masked_flat = masked.reshape(-1, channels)
    grad_second = lax.dot_general(
        patches_second, masked_flat, (((0,), (0,)), ((), ())), preferred_element_type=jnp.float32
    )
    grad_rims = jnp.stack([masked[:, 0], masked[:, :, 0]], axis=1)
    all_grads = lax.all_gather(grad_rims, "region", axis=0, tiled=True)
    grad_below = fetch(all_grads, 1, 0, 0)
    grad_right = fetch(all_grads, 0, 1, 1)
    grad_corner = fetch(all_grads, 1, 1, 0)[:, 0]
    grad_body = jnp.concatenate([masked, grad_right[:, :, None]], axis=2)
    grad_bottom = jnp.concatenate([grad_below, grad_corner[:, None]], axis=1)
    grad_pad = jnp.concatenate([grad_body, grad_bottom[:, None]], axis=1)
    extended = tile_half + 1
    spread = lax.dot_general(
        grad_pad.reshape(-1, channels),
        second_full,
        (((1,), (1,)), ((), ())),
        preferred_element_type=jnp.float32,
    )
    spread = spread.reshape(slot_count, extended, extended, 3, 3, channels)
    row_even = spread[:, :, :, 0] + shift_down(spread[:, :, :, 2], 1)
    row_odd = spread[:, :, :, 1]
    by_rows = jnp.stack([row_even, row_odd], axis=2).reshape(
        slot_count, 2 * extended, extended, 3, channels
    )
    col_even = by_rows[:, :, :, 0] + shift_down(by_rows[:, :, :, 2], 2)
    col_odd = by_rows[:, :, :, 1]
    dense = jnp.stack([col_even, col_odd], axis=3).reshape(
        slot_count, 2 * extended, 2 * extended, channels
    )
    dhidden = dense[:, 1 : tile_side + 1, 1 : tile_side + 1]
    dpre = (dhidden * silu_slope(pre_act)).astype(jnp.bfloat16)
    grad_first = lax.dot_general(
        patches_first,
        dpre.reshape(-1, channels),
        (((0,), (0,)), ((), ())),
        preferred_element_type=jnp.float32,
    )
    row_block = grad_first.shape[0] // lax.axis_size("region")
    full_first, full_second = lax.psum((grad_first, grad_second), "region")
    sum_sq = jnp.sum(full_first * full_first) + jnp.sum(full_second * full_second)
    row_start = lax.axis_index("region") * row_block
    share_first = lax.dynamic_slice_in_dim(full_first, row_start, row_block, 0)
    share_second = lax.dynamic_slice_in_dim(full_second, row_start, row_block, 0)
    factor = 3.0 * channels * math.sqrt(2.0) / (jnp.sqrt(sum_sq) + 0.01) / lax.axis_size("scene")
    out_first, out_second = (
        lax.psum_scatter(factor * share_first, "scene", scatter_dimension=1, tiled=True),
        lax.psum_scatter(factor * share_second, "scene", scatter_dimension=1, tiled=True),
    )
    return (features, out_first, out_second)


def solution(mesh):
    in_specs = (
        P("scene", "region", None, None, None),
        P("scene", "region", None, None, None),
        P("scene", "region"),
        P("scene", "region"),
        P("scene", None),
        P("scene", None),
    )
    out_specs = (P("scene", "region", None, None, None), P("region", "scene"), P("region", "scene"))
    return jax.shard_map(local, mesh=mesh, in_specs=in_specs, out_specs=out_specs, check_vma=False)
```

profile of v0, /device:TPU:1, one launch (start us, length us, event | category | flops | bytes accessed | tf_op | source)
XLA Modules:
  0.0 680.4 jit_solution(13259119407148330793)
XLA Ops:
  17.6 20.5 %all-reduce.2 = s32[64]{0:T(128)S(1)} all-reduce(s32[64]{0:T(128)S(1)} %bitcast_dynamic-update-slice_fusion), channel_id=1, replica_groups=mesh['scene'=8,'region'=32] {'region'}, use_global_device_ids=true, to_apply=%add.2 | all-reduce | flops 64 | bytes 512
  48.8 37.5 %all-gather.14.cloned.1.call-done = bf16[64,2,16,256]{3,2,1,0:T(8,128)(2,1)} async-done(((bf16[2,2,16,256]{3,2,1,0:T(8,128)(2,1)}), bf16[64,2,16,256]{3,2,1,0:T(8,128)(2,1)}) %all-gather.14.cloned.1.call-update) | async-done | bytes 1048592 | tf_op jit(solution)/shard_map/all_gather | solution.py:111
  86.2 1.8 gather_fusion.21
  88.1 1.8 gather_fusion.19
  90.1 1.8 gather_fusion.20
  92.0 78.7 %all-gather.6.cloned.1.call-done = bf16[64,4,32,256]{3,2,1,0:T(8,128)(2,1)} async-done(((bf16[2,4,32,256]{3,2,1,0:T(8,128)(2,1)}), bf16[64,4,32,256]{3,2,1,0:T(8,128)(2,1)}) %all-gather.6.cloned.1.call-update) | async-done | bytes 4194320 | tf_op jit(solution)/shard_map/all_gather | solution.py:72
  170.7 2.7 gather_fusion.15
  174.1 24.9 %all-gather.12.cloned.1.call-done = bf16[2304,256]{1,0:T(8,128)(2,1)} async-done(((bf16[288,256]{1,0:T(8,128)(2,1)}), bf16[2304,256]{1,0:T(8,128)(2,1)}) %all-gather.12.cloned.1.call-update) | async-done | bytes 1179664 | tf_op jit(solution)/shard_map/all_gather | solution.py:91
  199.0 2.5 fusion.11
  201.8 1.8 fusion.1
  203.6 3.6 gather_fusion.13
  208.6 3.5 gather_fusion.9
  214.3 3.5 gather_fusion.1
  219.9 3.6 gather_fusion.5
  225.6 3.5 gather_fusion.11
  231.2 3.5 gather_fusion.7
  237.0 3.5 gather_fusion.3
  242.9 2.8 pad_maximum_fusion.2
  247.3 3.6 copy.128
  250.9 3.7 copy.138
  254.6 1.6 slice_dynamic-update-slice_fusion.4
  256.2 1.6 slice_dynamic-update-slice_fusion.3
  257.9 1.6 fusion.9
  260.6 1.7 fusion.8
  263.4 1.7 slice_dynamic-update-slice_fusion.1
  266.7 8.0 %multiply_convert_fusion = (bf16[2,32,32,256]{3,2,1,0:T(8,128)(2,1)S(1)}, f32[2,32,32,256]{3,2,1,0:T(8,128)}) fusion(bf16[2,32,32,2304]{3,2,1,0:T(8,128)(2,1)} %slice_dynamic-update-slice_fusion, bf16[2304,256]{1,0:T(8,128)(2,1)} %all-gather.8.cloned.1.call-done), kind=kOutput, calls=%fused_computation.36 | convolution fusion | flops 2418540544 | bytes 13762560 | tf_op jit(solution)/shard_map/dot_general | solution.py:86
  274.8 9.9 %slice.204 = bf16[2,16,16,256]{3,2,1,0:T(8,128)(2,1)} slice(bf16[2,32,32,256]{3,2,1,0:T(8,128)(2,1)S(1)} %get-tuple-element.70), slice={[0:2:1], [0:32:2], [0:32:2], [0:256:1]} | slice | bytes 524288 | tf_op jit(solution)/shard_map/slice | solution.py:21
  284.7 9.8 %slice.205 = bf16[2,16,16,256]{3,2,1,0:T(8,128)(2,1)} slice(bf16[2,32,32,256]{3,2,1,0:T(8,128)(2,1)S(1)} %get-tuple-element.70), slice={[0:2:1], [0:32:2], [1:32:2], [0:256:1]} | slice | bytes 524288 | tf_op jit(solution)/shard_map/slice | solution.py:21
  294.5 9.8 %slice.207 = bf16[2,16,16,256]{3,2,1,0:T(8,128)(2,1)} slice(bf16[2,32,32,256]{3,2,1,0:T(8,128)(2,1)S(1)} %get-tuple-element.70), slice={[0:2:1], [1:32:2], [0:32:2], [0:256:1]} | slice | bytes 524288 | tf_op jit(solution)/shard_map/slice | solution.py:21
  304.4 9.8 %slice.208 = bf16[2,16,16,256]{3,2,1,0:T(8,128)(2,1)} slice(bf16[2,32,32,256]{3,2,1,0:T(8,128)(2,1)S(1)} %get-tuple-element.70), slice={[0:2:1], [1:32:2], [1:32:2], [0:256:1]} | slice | bytes 524288 | tf_op jit(solution)/shard_map/slice | solution.py:21
  314.2 2.4 slice_bitcast_fusion.3
  317.3 2.2 fusion.4
  322.2 7.9 %convolution_bitcast_fusion.1 = f32[2304,256]{1,0:T(8,128)} fusion(bf16[2,32,32,2304]{3,2,1,0:T(8,128)(2,1)} %slice_dynamic-update-slice_fusion, f32[2,32,32,256]{3,0,2,1:T(2,128)S(1)} %slice.308, f32[2,32,32,256]{3,2,1,0:T(8,128)S(1)} %copy-done.25), kind=kOutput, calls=%fused_computation.24 | convolution fusion | flops 2420637696 | bytes 15990784 | tf_op jit(solution)/shard_map/dot_general | solution.py:138
  330.2 61.1 %all-gather.10.cloned.1.call-done = bf16[64,2,32,256]{3,2,1,0:T(8,128)(2,1)} async-done(((bf16[2,2,32,256]{3,2,1,0:T(8,128)(2,1)}), bf16[64,2,32,256]{3,2,1,0:T(8,128)(2,1)}) %all-gather.10.cloned.1.call-update) | async-done | bytes 2097168 | tf_op jit(solution)/shard_map/all_gather | solution.py:95
  391.3 2.3 gather_fusion.18
  393.7 1.8 pad_maximum_fusion.3
  395.6 2.3 gather_fusion.16
  398.0 2.3 gather_fusion.17
  403.9 12.5 %slice.203 = bf16[2,16,16,256]{3,2,1,0:T(8,128)(2,1)S(1)} slice(bf16[2,32,33,256]{3,2,1,0:T(8,128)(2,1)} %pad_maximum_fusion.3), slice={[0:2:1], [0:32:2], [0:32:2], [0:256:1]} | slice | bytes 524288 | tf_op jit(solution)/shard_map/slice | solution.py:21
  416.5 12.5 %slice.206 = bf16[2,16,16,256]{3,2,1,0:T(8,128)(2,1)S(1)} slice(bf16[2,32,33,256]{3,2,1,0:T(8,128)(2,1)} %pad_maximum_fusion.3), slice={[0:2:1], [1:32:2], [0:32:2], [0:256:1]} | slice | bytes 524288 | tf_op jit(solution)/shard_map/slice | solution.py:21
  430.7 2.3 convolution_bitcast_fusion
  433.1 167.9 %all-reduce.6.cloned.1.call-done = (f32[2304,256]{1,0:T(8,128)}, f32[2304,256]{1,0:T(8,128)}) async-done(((f32[2304,256]{1,0:T(8,128)}, f32[2304,256]{1,0:T(8,128)}), (f32[2304,256]{1,0:T(8,128)}, f32[2304,256]{1,0:T(8,128)})) %all-reduce.6.cloned.1.call-update) | async-done | bytes 4718608 | tf_op jit(solution)/shard_map/psum | solution.py:145
  601.0 3.0 multiply_reduce_fusion
  608.2 1.6 copy.141
  610.5 1.6 copy.139
  612.2 3.1 convolution_convert_fusion
  615.3 23.4 %reduce-scatter.9.cloned.1.call-done = f32[32,72]{1,0:T(8,128)} async-done(((f32[256,72]{1,0:T(8,128)}), f32[32,72]{1,0:T(8,128)}) %reduce-scatter.9.cloned.1.call-update) | async-done | bytes 9232
  638.8 34.8 %reduce-scatter.7.cloned.1.call-done = f32[32,72]{1,0:T(8,128)} async-done(((f32[256,72]{1,0:T(8,128)}), f32[32,72]{1,0:T(8,128)}) %reduce-scatter.7.cloned.1.call-update) | async-done | bytes 9232
  (169 shorter events, 54.0 us)
Async XLA Ops:
  7.2 79.1 %all-gather.14.cloned.1.call-start = ((), (), s32[]{:S(2)}) async-start(), calls=%async_computation.6 | async-start | bytes 1081344 | tf_op jit(solution)/shard_map/all_gather | solution.py:111
  8.9 190.1 %copy-start.3 = (bf16[2,16,16,256]{3,2,1,0:T(8,128)(2,1)}, bf16[2,16,16,256]{3,2,1,0:T(8,128)(2,1)S(1)}, u32[]{:S(2)}) copy-start(bf16[2,16,16,256]{3,2,1,0:T(8,128)(2,1)S(1)} %bitcast_multiply_fusion) | copy-start | bytes 786436
  9.7 161.0 %all-gather.6.cloned.1.call-start = ((), (), s32[]{:S(2)}) async-start(), calls=%async_computation.2 | async-start | bytes 4325376 | tf_op jit(solution)/shard_map/all_gather | solution.py:72
  12.4 186.6 %all-gather.12.cloned.1.call-start = ((), (), s32[]{:S(2)}) async-start(), calls=%async_computation.5 | async-start | bytes 1327104 | tf_op jit(solution)/shard_map/all_gather | solution.py:91
  13.1 253.6 %all-gather.8.cloned.1.call-start = ((), (), s32[]{:S(2)}) async-start(), calls=%async_computation.3 | async-start | bytes 1327104 | tf_op jit(solution)/shard_map/all_gather | solution.py:88
  13.7 377.6 %all-gather.10.cloned.1.call-start = ((), (), s32[]{:S(2)}) async-start(), calls=%async_computation.4 | async-start | bytes 2162688 | tf_op jit(solution)/shard_map/all_gather | solution.py:95
  39.6 52.4 %copy-start.20 = (pred[2]{0:T(512)(128)(4,1)}, pred[2]{0:T(512)(128)(4,1)S(1)}, u32[]{:S(2)}) copy-start(pred[2]{0:T(512)(128)(4,1)S(1)} %get-tuple-element.74) | copy-start | bytes 10
  40.8 51.0 %copy-start.21 = (bf16[2]{0:T(256)(128)(2,1)}, bf16[2]{0:T(256)(128)(2,1)S(1)}, u32[]{:S(2)}) copy-start(bf16[2]{0:T(256)(128)(2,1)S(1)} %get-tuple-element.78) | copy-start | bytes 16
  40.8 51.0 %copy-start.22 = (pred[2]{0:T(512)(128)(4,1)}, pred[2]{0:T(512)(128)(4,1)S(1)}, u32[]{:S(2)}) copy-start(pred[2]{0:T(512)(128)(4,1)S(1)} %get-tuple-element.41) | copy-start | bytes 10
  40.8 51.1 %copy-start.23 = (bf16[2]{0:T(256)(128)(2,1)}, bf16[2]{0:T(256)(128)(2,1)S(1)}, u32[]{:S(2)}) copy-start(bf16[2]{0:T(256)(128)(2,1)S(1)} %get-tuple-element.82) | copy-start | bytes 16
  40.8 51.0 %copy-start.14 = (s32[1024]{0:T(1024)}, s32[1024]{0:T(1024)S(1)}, u32[]{:S(2)}) copy-start(s32[1024]{0:T(1024)S(1)} %pad_clamp_fusion.2) | copy-start | bytes 12292
  40.9 49.0 %copy-start.13 = (s32[1024]{0:T(1024)}, s32[1024]{0:T(1024)S(1)}, u32[]{:S(2)}) copy-start(s32[1024]{0:T(1024)S(1)} %pad_clamp_fusion.6) | copy-start | bytes 12292
  203.6 39.3 %copy-start = (bf16[1,2,32,32,256]{4,3,2,1,0:T(8,128)(2,1)S(1)}, bf16[1,2,32,32,256]{4,3,2,1,0:T(8,128)(2,1)}, u32[]{:S(2)}) copy-start(bf16[1,2,32,32,256]{4,3,2,1,0:T(8,128)(2,1)} %param.14) | copy-start | bytes 3145732
  242.8 4.1 copy-start.1
  254.6 3.3 copy-start.11
  257.9 2.7 copy-start.10
  317.3 283.7 %all-reduce.6.cloned.1.call-start = ((), (), s32[]{:S(2)}) async-start(), calls=%async_computation.9 | async-start | bytes 9437184 | tf_op jit(solution)/shard_map/psum | solution.py:145
  320.6 1.6 copy-start.25
  322.2 71.3 %copy-start.19 = (pred[2]{0:T(512)(128)(4,1)S(1)}, pred[2]{0:T(512)(128)(4,1)}, u32[]{:S(2)}) copy-start(pred[2]{0:T(512)(128)(4,1)} %get-tuple-element.39) | copy-start | bytes 10
  322.2 71.4 %copy-start.17 = (bf16[2]{0:T(256)(128)(2,1)S(1)}, bf16[2]{0:T(256)(128)(2,1)}, u32[]{:S(2)}) copy-start(bf16[2]{0:T(256)(128)(2,1)} %get-tuple-element.81) | copy-start | bytes 16
  330.2 67.7 %copy-start.18 = (pred[2]{0:T(512)(128)(4,1)S(1)}, pred[2]{0:T(512)(128)(4,1)}, u32[]{:S(2)}) copy-start(pred[2]{0:T(512)(128)(4,1)} %get-tuple-element.33) | copy-start | bytes 10
  330.2 67.8 %copy-start.24 = (bf16[2]{0:T(256)(128)(2,1)S(1)}, bf16[2]{0:T(256)(128)(2,1)}, u32[]{:S(2)}) copy-start(bf16[2]{0:T(256)(128)(2,1)} %get-tuple-element.80) | copy-start | bytes 16
  330.2 70.1 %copy-start.15 = (pred[2]{0:T(512)(128)(4,1)S(1)}, pred[2]{0:T(512)(128)(4,1)}, u32[]{:S(2)}) copy-start(pred[2]{0:T(512)(128)(4,1)} %get-tuple-element.35) | copy-start | bytes 10
  330.2 70.1 %copy-start.16 = (bf16[2]{0:T(256)(128)(2,1)S(1)}, bf16[2]{0:T(256)(128)(2,1)}, u32[]{:S(2)}) copy-start(bf16[2]{0:T(256)(128)(2,1)} %get-tuple-element.76) | copy-start | bytes 16
  401.1 28.0 %copy-start.9 = (bf16[2,16,16,256]{3,2,1,0:T(8,128)(2,1)S(1)}, bf16[2,16,16,256]{3,2,1,0:T(8,128)(2,1)}, u32[]{:S(2)}) copy-start(bf16[2,16,16,256]{3,2,1,0:T(8,128)(2,1)} %slice.204) | copy-start | bytes 786436
  402.0 27.2 %copy-start.8 = (bf16[2,16,16,256]{3,2,1,0:T(8,128)(2,1)S(1)}, bf16[2,16,16,256]{3,2,1,0:T(8,128)(2,1)}, u32[]{:S(2)}) copy-start(bf16[2,16,16,256]{3,2,1,0:T(8,128)(2,1)} %slice.205) | copy-start | bytes 786436
  403.9 25.3 %copy-start.7 = (bf16[2,16,16,256]{3,2,1,0:T(8,128)(2,1)S(1)}, bf16[2,16,16,256]{3,2,1,0:T(8,128)(2,1)}, u32[]{:S(2)}) copy-start(bf16[2,16,16,256]{3,2,1,0:T(8,128)(2,1)} %slice.207) | copy-start | bytes 786436
  416.5 12.8 %copy-start.6 = (bf16[2,16,16,256]{3,2,1,0:T(8,128)(2,1)S(1)}, bf16[2,16,16,256]{3,2,1,0:T(8,128)(2,1)}, u32[]{:S(2)}) copy-start(bf16[2,16,16,256]{3,2,1,0:T(8,128)(2,1)} %slice.208) | copy-start | bytes 786436
  429.0 1.7 copy-start.4
  429.3 1.4 copy-start.12
  433.1 205.7 %reduce-scatter.9.cloned.1.call-start = ((), (), s32[]{:S(2)}) async-start(), calls=%async_computation.8 | async-start | bytes 147456
  601.0 3.0 copy-start.2
  601.0 11.2 %copy-start.5 = (bf16[2304,256]{1,0:T(8,128)(2,1)S(1)}, bf16[2304,256]{1,0:T(8,128)(2,1)}, u32[]{:S(2)}) copy-start(bf16[2304,256]{1,0:T(8,128)(2,1)} %all-gather.12.cloned.1.call-done) | copy-start | bytes 3538948
  609.8 63.8 %reduce-scatter.7.cloned.1.call-start = ((), (), s32[]{:S(2)}) async-start(), calls=%async_computation.7 | async-start | bytes 147456
Sparse Core Ops, SparseCore 0:
  10.6 75.6 all-gather.13
  89.4 81.2 all-gather.5
  172.5 26.4 all-gather.11
  200.7 26.2 all-gather.7
  317.4 73.7 all-gather.9
  433.2 167.7 all-reduce.5
  609.9 28.7 reduce-scatter.8
  641.8 31.7 reduce-scatter.6
where the time goes:
time: 686 us; the launch traced here: 680 us
  waiting for transfers between devices  430 us (63%)
  local copies, waits for them, and re-layouts  143 us (21%)
  other arithmetic  46.8 us (7%)
  matrix products  23.8 us (3%)
  blocking collectives  20.5 us (3%)
  between operations  16.8 us (2%)
    psum x1, waiting for transfers between devices, local(): full_first, full_second = lax.psum((grad_first, grad_second), 'region')  168 us
    all_gather x1, waiting for transfers between devices, local(): all_edges = lax.all_gather(edge_rims, 'region', axis=0, tiled=True)  78.7 us
    slice x9, local copies, waits for them, and re-layouts, tap_patches(): padded[:, tap_row:tap_row + stride * out_side:stride, tap_col:tap_col + s...  67.2 us
    all_gather x1, waiting for transfers between devices, local(): all_hidden = lax.all_gather(hidden_rims, 'region', axis=0, tiled=True)  61.1 us
    unnamed x10, waiting for transfers between devices  59.6 us
    gather x22, local copies, waits for them, and re-layouts, fetch(): picked = jnp.take(all_rims, jnp.take(slot_of, position), axis=0)[:, which]  44.7 us
    all_gather x1, waiting for transfers between devices, local(): all_grads = lax.all_gather(grad_rims, 'region', axis=0, tiled=True)  37.5 us
    all_gather x1, waiting for transfers between devices, local(): second_full = lax.all_gather(w_second, 'scene', axis=0, tiled=True)  24.9 us
  transfers between devices with their start and end apart: 8, of which 7 were waited for; matrix products, arithmetic and copies ran while one was open for 16% of the time, Pallas kernels for 0%

commit v1 on v0

v1 whole, which is shorter than its diff:
```python
import math

import jax
import jax.numpy as jnp
import ml_dtypes
import numpy as np
from jax import lax
from jax.experimental import pallas as pl
from jax.experimental.pallas import tpu as pltpu
from jax.sharding import PartitionSpec as P

MESH = pl.DeviceIdType.MESH
BF = jnp.bfloat16
F32 = jnp.float32
GW, GH = 4, 16
C = 256
REG, ZN, YN, SC = 32, 8, 4, 8
WROWS = 288
LEFT = 48
VMEM_LIMIT = 56 * 1024 * 1024


def hot(rows, cols, pairs):
    out = np.zeros((rows, cols), np.float32)
    for row, col in pairs:
        out[row, col] = 1.0
    return out.astype(ml_dtypes.bfloat16)


def halo_row(k, t, q):
    return k * 16 + t * 8 + q


def place_tables():
    cols = lambda blk, b: 2 * b - 1 + blk
    body = hot(512, 256, [
        (blk * 128 + h * 16 + b, h * 32 + cols(blk, b))
        for blk in range(4) for h in range(8) for b in range(16) if 0 <= cols(blk, b) < 32
    ])
    sides = np.stack([
        hot(512, 128, [(h * 16, halo_row(h, t, 2)) for h in range(8)]
            + [(3 * 128 + h * 16 + 15, halo_row(h, t, 5)) for h in range(8)])
        for t in range(2)
    ])
    edge_q = (1, 0, 4)
    corner_left, corner_right = (1, 3, 7), (4, 5, 8)

    def edge_source(t, sel, col):
        if col < 0:
            return halo_row(corner_left[sel], t, 7)
        if col > 31:
            return halo_row(corner_right[sel], t, 7)
        return halo_row(col, t, edge_q[sel])

    edges = np.stack([
        hot(192, 512, [
            (sel * 64 + blk * 16 + b, edge_source(t, sel, cols(blk, b)))
            for sel in range(3) for blk in range(4) for b in range(16)
        ])
        for t in range(2)
    ])

    def left_source(t, hh, j):
        if 0 <= hh < 32:
            return halo_row(hh, t, (3, 2)[j]) if j < 2 else None
        sel = {-2: 0, -1: 1, 32: 2}[hh]
        if j < 2:
            return halo_row(((0, 1), (2, 3), (6, 7))[sel][j], t, 7)
        return halo_row(0, t, edge_q[sel])

    left = np.stack([
        hot(9 * LEFT, 512, [
            ((3 * i + j) * LEFT + g, left_source(t, g + i - 2, j))
            for i in range(3) for j in range(3) for g in range(33)
            if left_source(t, g + i - 2, j) is not None
        ])
        for t in range(2)
    ])
    first_col = hot(3 * LEFT, 1024, [
        (i * LEFT + g, (g + i - 2) * 32) for i in range(3) for g in range(33) if 0 <= g + i - 2 < 32
    ])
    shift = hot(272, 272, [(a * 16 + b, a * 16 + b - 1) for a in range(17) for b in range(1, 16)])
    from_left = np.stack([
        hot(272, 2 * LEFT, [
            (a * 16, t * LEFT + 2 * a + par) for a in range(17 - par)
        ])
        for t in range(2) for par in range(2)
    ])
    back = hot(272, 256, [(a * 16 + b, a * 16 + b + 1) for a in range(16) for b in range(15)])
    below = np.stack([hot(16, 512, [(b, halo_row(b, t, 6)) for b in range(16)]) for t in range(2)])
    beside = np.stack([
        hot(272, 512, [(a * 16 + 15, halo_row(16 + a, t, 6)) for a in range(16)]
            + [(256 + b, halo_row(b + 1, t, 6)) for b in range(15)] + [(271, halo_row(9, t, 7))])
        for t in range(2)
    ])
    return body, sides, edges, left, first_col, shift, from_left, back, below, beside


def dot(a, b):
    return jnp.dot(a, b, preferred_element_type=F32)


def dot_t(a, b):
    return lax.dot_general(a, b, (((1,), (1,)), ((), ())), preferred_element_type=F32)


def exchange_kernel(send1, w1, w2, halo_out, w1_out, w2_out,
                    recv1, send2, recv2, s1, r1, s2, r2, ws, wr, fs, fr, ls):
    s = lax.axis_index("scene")
    r = lax.axis_index("region")
    sib = s + 1 - 2 * (s % 2)

    barrier = pltpu.get_barrier_semaphore()

    def greet(o, carry):
        pl.semaphore_signal(barrier, inc=1, device_id={"region": (r + o) % REG}, device_id_type=MESH)
        return carry

    lax.fori_loop(1, REG, greet, 0)
    for o in range(1, 4):
        pl.semaphore_signal(barrier, inc=1, device_id={"scene": (s + 2 * o) % SC}, device_id_type=MESH)
    pl.semaphore_signal(barrier, inc=1, device_id={"scene": sib}, device_id_type=MESH)
    pl.semaphore_wait(barrier, REG - 1 + 4)

    def first(o, carry):
        to = (r + o) % REG
        pltpu.make_async_remote_copy(
            src_ref=send1.at[to], dst_ref=recv1.at[r], send_sem=s1, recv_sem=r1,
            device_id={"region": to}, device_id_type=MESH).start()
        return carry

    lax.fori_loop(1, REG, first, 0)
    weights = ((w1, w1_out), (w2, w2_out))
    far = []
    near = []
    own = []
    for n, (src, dst) in enumerate(weights):
        for o in range(1, 4):
            far.append(pltpu.make_async_remote_copy(
                src_ref=src, dst_ref=dst.at[s], send_sem=ws.at[n, o - 1], recv_sem=wr.at[n, o - 1],
                device_id={"scene": (s + 2 * o) % SC}, device_id_type=MESH))
        near.append(pltpu.make_async_remote_copy(
            src_ref=src, dst_ref=dst.at[s], send_sem=fs.at[n, 0], recv_sem=fr.at[n, 0],
            device_id={"scene": sib}, device_id_type=MESH))
        own.append(pltpu.make_async_copy(src, dst.at[s], ls.at[n]))
    for copy in far + near + own:
        copy.start()

    recv1[r] = send1[r]
    pltpu.make_async_copy(recv1.at[pl.ds(0, REG - 1)], recv1.at[pl.ds(0, REG - 1)], r1).wait()

    held = recv1[...].reshape(512, 384)
    pixels = held[:, :256]
    pos = held[:, 256:].astype(F32)
    lane = lax.broadcasted_iota(jnp.int32, (512, 128), 1).astype(F32)
    q = lax.broadcasted_iota(jnp.int32, (512, 128), 0) % 8
    zero = jnp.zeros((512, 128), F32)
    k = zero.astype(jnp.int32) + r
    grad_row = jnp.where(k < 16, 1.0, 0.0)
    corner_row = jnp.where(k < 6, -1.0, 1.0)
    corner_col = jnp.where((k < 4) | (k == 6) | (k == 7), -1.0, 1.0)
    d_row = jnp.where(q < 2, -1.0, jnp.where(q == 4, 1.0, zero))
    d_row = jnp.where(q == 6, grad_row, jnp.where(q == 7, corner_row, d_row))
    d_col = jnp.where((q == 2) | (q == 3), -1.0, jnp.where(q == 5, 1.0, zero))
    d_col = jnp.where(q == 6, 1.0 - grad_row, jnp.where(q == 7, corner_col, d_col))
    p_row = jnp.floor(pos * 0.25)
    n_row = p_row + d_row
    n_col = pos - 4.0 * p_row + d_col
    inside = (n_row >= 0.0) & (n_row < GH) & (n_col >= 0.0) & (n_col < GW)
    want = jnp.where(inside, 4.0 * n_row + n_col, -1.0)
    has = jnp.where(pos == lane, 1.0, 0.0).astype(BF)
    wants = jnp.where(want == lane, 1.0, 0.0).astype(BF)
    same = (lax.broadcasted_iota(jnp.int32, (512, 512), 0) % 8) == (
        lax.broadcasted_iota(jnp.int32, (512, 512), 1) % 8)
    route = jnp.where(same, dot_t(wants, has), 0.0).astype(BF)
    send2[...] = dot(route, pixels).astype(BF).reshape(REG, 16, 256)

    def second(o, carry):
        to = (r + o) % REG
        pltpu.make_async_remote_copy(
            src_ref=send2.at[to], dst_ref=recv2.at[r], send_sem=s2, recv_sem=r2,
            device_id={"region": to}, device_id_type=MESH).start()
        return carry

    lax.fori_loop(1, REG, second, 0)
    recv2[r] = send2[r]

    forward = []
    for o in range(1, 4):
        came = (s - 2 * o + SC) % SC
        for n, (src, dst) in enumerate(weights):
            far[3 * n + o - 1].wait_recv()
            copy = pltpu.make_async_remote_copy(
                src_ref=dst.at[came], dst_ref=dst.at[came], send_sem=fs.at[n, o], recv_sem=fr.at[n, o],
                device_id={"scene": sib}, device_id_type=MESH)
            copy.start()
            forward.append(copy)
    pltpu.make_async_copy(recv2.at[pl.ds(0, REG - 1)], recv2.at[pl.ds(0, REG - 1)], r2).wait()
    halo_out[...] = recv2[...]
    for copy in near + forward:
        copy.wait_recv()
    for copy in own:
        copy.wait()
    for copy in far + near + forward:
        copy.wait_send()
    pltpu.make_async_copy(send1.at[pl.ds(0, REG - 1)], send1.at[pl.ds(0, REG - 1)], s1).wait()
    pltpu.make_async_copy(send2.at[pl.ds(0, REG - 1)], send2.at[pl.ds(0, REG - 1)], s2).wait()


def exchange(send1, w1, w2):
    vmem = pl.BlockSpec(memory_space=pltpu.VMEM)
    anywhere = pl.BlockSpec(memory_space=pl.ANY)
    full = jax.ShapeDtypeStruct((SC, WROWS, C), BF)
    return pl.pallas_call(
        exchange_kernel,
        name="exchange",
        out_shape=(jax.ShapeDtypeStruct((REG, 16, C), BF), full, full),
        in_specs=[vmem, anywhere, anywhere],
        out_specs=(vmem, anywhere, anywhere),
        scratch_shapes=[
            pltpu.VMEM((REG, 16, 384), BF),
            pltpu.VMEM((REG, 16, C), BF),
            pltpu.VMEM((REG, 16, C), BF),
            pltpu.SemaphoreType.DMA, pltpu.SemaphoreType.DMA,
            pltpu.SemaphoreType.DMA, pltpu.SemaphoreType.DMA,
            pltpu.SemaphoreType.DMA((2, 3)), pltpu.SemaphoreType.DMA((2, 3)),
            pltpu.SemaphoreType.DMA((2, 4)), pltpu.SemaphoreType.DMA((2, 4)),
            pltpu.SemaphoreType.DMA((2,)),
        ],
        compiler_params=pltpu.CompilerParams(
            collective_id=0, has_side_effects=True, vmem_limit_bytes=VMEM_LIMIT),
    )(send1, w1, w2)


def sigmoid(v):
    return 1.0 / (1.0 + jnp.exp(-v))


def compute_kernel(pos, tiles, masked, halo, w1, w2, body, sides, edges, left, first_col, shift,
                   from_left, back, below, beside, feat, grads,
                   x4, h_odd, h_even, left_x, grad_t, g_both):
    halo_px = halo[...].reshape(512, C)
    for t in range(2):
        for c in range(4):
            chunk = tiles[t, 8 * c:8 * c + 8].reshape(256, C)
            got = dot(body[...], chunk) + dot(sides[t], halo[8 * c:8 * c + 8].reshape(128, C))
            got = got.astype(BF)
            for blk in range(4):
                x4[t, 4 * c + 1:4 * c + 5, :, :, blk * C:(blk + 1) * C] = (
                    got[blk * 128:(blk + 1) * 128].reshape(4, 2, 16, C))
        rim = dot(edges[t], halo_px).astype(BF)
        for sel, (pair, par) in enumerate(((0, 0), (0, 1), (17, 0))):
            for blk in range(4):
                start = sel * 64 + blk * 16
                x4[t, pair, par, :, blk * C:(blk + 1) * C] = rim[start:start + 16]
        side = dot(left[t], halo_px)
        inner = dot(first_col[...], tiles[t].reshape(1024, C))
        for i in range(3):
            for j in range(3):
                tap = 3 * i + j
                part = side[tap * LEFT:(tap + 1) * LEFT]
                if j == 2:
                    part = part + inner[i * LEFT:(i + 1) * LEFT]
                left_x[t * LEFT:(t + 1) * LEFT, tap * C:(tap + 1) * C] = part.astype(BF)

    pre_left = dot(left_x[...], w1[...])
    row_id = lax.broadcasted_iota(jnp.int32, (LEFT, C), 0)
    kept = []
    above = []
    for t in range(2):
        here = pos[0, t]
        has_left = jnp.where(here % GW > 0, 1.0, 0.0)
        has_above = jnp.where(here >= GW, 1.0, 0.0)
        above.append(has_above)
        v = pre_left[t * LEFT:(t + 1) * LEFT]
        keep = jnp.where(row_id == 0, has_left * has_above, has_left)
        kept.append((v * sigmoid(v) * keep).astype(BF))
    hidden_left = jnp.concatenate(kept, axis=0)

    m_t = jnp.concatenate(
        [masked[t].reshape(256, C).astype(F32).T.astype(BF) for t in range(2)], axis=1)

    def window(t, par, i, cp, lo):
        row = 2 * lo + par + i
        n = 17 if (par == 0 and lo == 0) else 16
        return x4[t, row // 2:row // 2 + n, row % 2, :, cp * C:cp * C + 768].reshape(n * 16, 768)

    for t in range(2):
        m0 = masked[t].reshape(256, C)
        m0 = jnp.concatenate([m0, dot(below[t], halo_px).astype(BF)], axis=0)
        m1 = (dot(back[...], m0[:256]) + dot(beside[t], halo_px)).astype(BF)

        def second(tap):
            return w2[tap * C:(tap + 1) * C, :]

        up, down = slice(0, 256), slice(16, 272)
        spread = {
            (1, 0): lambda: dot_t(m0[up], second(4)),
            (1, 1): lambda: dot_t(m0[up], second(5)) + dot_t(m1[up], second(3)),
            (0, 0): lambda: dot_t(m0[up], second(7)) + dot_t(m0[down], second(1)),
            (0, 1): lambda: (dot_t(m0[up], second(8)) + dot_t(m1[up], second(6))
                             + dot_t(m0[down], second(2)) + dot_t(m1[down], second(0))),
        }
        for par in range(2):
            store = h_odd if par == 0 else h_even
            n = 17 - par
            for cp in range(2):
                patch = jnp.concatenate([window(t, par, i, cp, 0) for i in range(3)], axis=1)
                pre = dot(patch, w1[...])
                sig = sigmoid(pre)
                act = pre * sig
                if par == 0:
                    own_row = lax.broadcasted_iota(jnp.int32, (272, C), 0) >= 16
                    act = jnp.where(own_row, act, act * above[t])
                act = act.astype(BF)
                if cp == 0:
                    store[t, :, :, C:2 * C] = act.reshape(n, 16, C)
                else:
                    store[t, :, :, 2 * C:] = act.reshape(n, 16, C)
                    moved = dot(shift[:n * 16, :n * 16], act)
                    moved = moved + dot(from_left[2 * t + par][:n * 16], hidden_left)
                    store[t, :, :, :C] = moved.astype(BF).reshape(n, 16, C)
                if par == 0:
                    pre, sig = pre[16:], sig[16:]
                slope = sig * (1.0 + pre * (1.0 - sig))
                d_pre = spread[par, cp]() * slope
                group = 4 * t + 2 * par + cp
                grad_t[:, group * 256:(group + 1) * 256] = d_pre.T.astype(BF)

    def hidden_rows(t, i):
        if i == 1:
            return h_even[t].reshape(256, 768)
        return h_odd[t, i // 2:i // 2 + 16].reshape(256, 768)

    for t in range(2):
        patch = jnp.concatenate([hidden_rows(t, i) for i in range(3)], axis=1)
        feat[t] = dot(patch, w2[...]).astype(BF).reshape(16, 16, C)

    def own_rows(t, par, i, cp, j):
        row = (2 if par == 0 else 1) + i
        lanes = (cp + j) * C
        return x4[t, row // 2:row // 2 + 16, row % 2, :, lanes:lanes + C].reshape(256, C)

    for i in range(3):
        for j in range(3):
            tap = 3 * i + j
            seen = jnp.concatenate([hidden_rows(t, i)[:, j * C:(j + 1) * C] for t in range(2)], axis=0)
            g_both[1, tap * C:(tap + 1) * C, :] = dot(m_t, seen).T
            seen = jnp.concatenate(
                [own_rows(t, par, i, cp, j) for t in range(2) for par in range(2) for cp in range(2)], axis=0)
            g_both[0, tap * C:(tap + 1) * C, :] = dot(grad_t[...], seen).T

    for y in range(YN):
        for z in range(ZN):
            start = 72 * (z * YN + y)
            both = jnp.concatenate([g_both[0, start:start + 72, :], g_both[1, start:start + 72, :]], axis=0)
            grads[y, z] = both.astype(BF)


def compute(pos, tiles, masked, halo, w1, w2):
    tables = place_tables()
    vmem = pl.BlockSpec(memory_space=pltpu.VMEM)
    return pl.pallas_call(
        compute_kernel,
        name="compute",
        out_shape=(jax.ShapeDtypeStruct((2, 16, 16, C), BF), jax.ShapeDtypeStruct((YN, ZN, 144, C), BF)),
        in_specs=[pl.BlockSpec(memory_space=pltpu.SMEM)] + [vmem] * 15,
        out_specs=(vmem, vmem),
        scratch_shapes=[
            pltpu.VMEM((2, 18, 2, 16, 4 * C), BF),
            pltpu.VMEM((2, 17, 16, 3 * C), BF),
            pltpu.VMEM((2, 16, 16, 3 * C), BF),
            pltpu.VMEM((2 * LEFT, 9 * C), BF),
            pltpu.VMEM((C, 2048), BF),
            pltpu.VMEM((2, 9 * C, C), F32),
        ],
        compiler_params=pltpu.CompilerParams(vmem_limit_bytes=VMEM_LIMIT),
    )(pos, tiles, masked, halo, w1, w2, *[jnp.asarray(table) for table in tables])


Z_ORDER = (4, 3, 5, 2, 6, 1, 7, 0)


def reduce_kernel(g, out, y_buf, z_send, z_buf, n_send, n_buf, x_send, x_buf,
                  ys, yr, zs, zr, ns, nr, xs, xr):
    s = lax.axis_index("scene")
    r = lax.axis_index("region")
    z, y = r // YN, r % YN

    def at_y(o):
        return {"region": z * YN + (y + o) % YN}

    def at_z(o):
        return {"region": ((z + o) % ZN) * YN + y}

    barrier = pltpu.get_barrier_semaphore()
    for o in range(1, YN):
        pl.semaphore_signal(barrier, inc=1, device_id=at_y(o), device_id_type=MESH)
    for o in range(1, ZN):
        pl.semaphore_signal(barrier, inc=1, device_id=at_z(o), device_id_type=MESH)
    for o in range(1, SC):
        pl.semaphore_signal(barrier, inc=1, device_id={"scene": (s + o) % SC}, device_id_type=MESH)
    pl.semaphore_wait(barrier, YN + ZN + SC - 3)

    y_copies = {}
    for oz in Z_ORDER:
        zz = (z + oz) % ZN
        for o in range(1, YN):
            copy = pltpu.make_async_remote_copy(
                src_ref=g.at[(y + o) % YN, zz], dst_ref=y_buf.at[o - 1, oz],
                send_sem=ys.at[o - 1, oz], recv_sem=yr.at[o - 1, oz],
                device_id=at_y(o), device_id_type=MESH)
            copy.start()
            y_copies[o, oz] = copy
    z_copies = []
    for oz in Z_ORDER:
        zz = (z + oz) % ZN
        total = g[y, zz].astype(F32)
        for o in range(1, YN):
            y_copies[o, oz].wait_recv()
            total = total + y_buf[o - 1, oz].astype(F32)
        if oz:
            z_send[oz - 1] = total.astype(BF)
            copy = pltpu.make_async_remote_copy(
                src_ref=z_send.at[oz - 1], dst_ref=z_buf.at[oz - 1],
                send_sem=zs.at[oz - 1], recv_sem=zr.at[oz - 1],
                device_id=at_z(oz), device_id_type=MESH)
            copy.start()
            z_copies.append(copy)
    for n, copy in enumerate(z_copies):
        copy.wait_recv()
        total = total + z_buf[Z_ORDER[n] - 1].astype(F32)

    squares = jnp.sum((total * total).reshape(18, 8, C), axis=0)
    n_send[0] = squares[:, :128] + squares[:, 128:]
    n_copies = []
    for o in range(1, YN):
        copy = pltpu.make_async_remote_copy(
            src_ref=n_send.at[0], dst_ref=n_buf.at[o - 1], send_sem=ns.at[o - 1], recv_sem=nr.at[o - 1],
            device_id=at_y(o), device_id_type=MESH)
        copy.start()
        n_copies.append(copy)
    turned = total.T
    part = n_send[0]
    for o in range(1, YN):
        n_copies[o - 1].wait_recv()
        part = part + n_buf[o - 1]
    n_send[1] = part
    for o in range(1, ZN):
        copy = pltpu.make_async_remote_copy(
            src_ref=n_send.at[1], dst_ref=n_buf.at[o + 2], send_sem=ns.at[o + 2], recv_sem=nr.at[o + 2],
            device_id=at_z(o), device_id_type=MESH)
        copy.start()
        n_copies.append(copy)
    for o in range(1, ZN):
        n_copies[o + 2].wait_recv()
        part = part + n_buf[o + 2]
    sum_sq = jnp.sum(part, keepdims=True)
    factor = (3.0 * C * math.sqrt(2.0) / SC) / (jnp.sqrt(sum_sq) + 0.01)
    x_send[...] = (turned * factor).reshape(SC, 32, 144)
    x_copies = []
    for o in range(1, SC):
        to = (s + o) % SC
        copy = pltpu.make_async_remote_copy(
            src_ref=x_send.at[to], dst_ref=x_buf.at[o - 1], send_sem=xs.at[o - 1], recv_sem=xr.at[o - 1],
            device_id={"scene": to}, device_id_type=MESH)
        copy.start()
        x_copies.append(copy)
    result = x_send[s]
    for o in range(1, SC):
        x_copies[o - 1].wait_recv()
        result = result + x_buf[o - 1]
    out[...] = result
    for copy in list(y_copies.values()) + z_copies + n_copies + x_copies:
        copy.wait_send()


def reduce(g):
    vmem = pl.BlockSpec(memory_space=pltpu.VMEM)
    dma = pltpu.SemaphoreType.DMA
    return pl.pallas_call(
        reduce_kernel,
        name="reduce",
        out_shape=jax.ShapeDtypeStruct((32, 144), F32),
        in_specs=[vmem],
        out_specs=vmem,
        scratch_shapes=[
            pltpu.VMEM((YN - 1, ZN, 144, C), BF),
            pltpu.VMEM((ZN - 1, 144, C), BF),
            pltpu.VMEM((ZN - 1, 144, C), BF),
            pltpu.VMEM((2, 8, 128), F32),
            pltpu.VMEM((YN + ZN - 2, 8, 128), F32),
            pltpu.VMEM((SC, 32, 144), F32),
            pltpu.VMEM((SC - 1, 32, 144), F32),
            dma((YN - 1, ZN)), dma((YN - 1, ZN)), dma((ZN - 1,)), dma((ZN - 1,)),
            dma((YN + ZN - 2,)), dma((YN + ZN - 2,)), dma((SC - 1,)), dma((SC - 1,)),
        ],
        compiler_params=pltpu.CompilerParams(
            collective_id=1, has_side_effects=True, vmem_limit_bytes=VMEM_LIMIT),
    )(g)


def local(tiles, cotangent, positions, clear, w_first, w_second):
    tiles_here = tiles[0]
    masked = cotangent[0] * clear[0].astype(BF)[:, None, None, None]
    grad_px = jnp.concatenate([masked[:, 0], masked[:, :, 0]], axis=1)
    corner = jnp.concatenate([
        tiles_here[:, 30:32, 30:32].reshape(2, 4, C),
        tiles_here[:, 30:32, 0],
        tiles_here[:, 0, 30:32],
        tiles_here[:, 0, 0:1],
        masked[:, 0, 0:1],
        jnp.zeros((2, 22, C), BF),
    ], axis=1)
    rims = jnp.stack([
        tiles_here[:, 31], tiles_here[:, 30], tiles_here[:, :, 31], tiles_here[:, :, 30],
        tiles_here[:, 0], tiles_here[:, :, 0], grad_px, corner,
    ], axis=2)
    rims = rims.transpose(1, 0, 2, 3).reshape(REG, 16, C)
    where = jnp.broadcast_to(positions[0].astype(BF)[None, :, None, None], (REG, 2, 8, 128))
    send1 = jnp.concatenate([rims, where.reshape(REG, 16, 128)], axis=2)
    halo, w1, w2 = exchange(send1, w_first, w_second)
    feat, grads = compute(
        positions, tiles_here, masked, halo, w1.reshape(9 * C, C), w2.reshape(9 * C, C))
    out = reduce(grads)
    return feat[None], out[:, :72].T, out[:, 72:].T


def solution(mesh):
    in_specs = (
        P("scene", "region", None, None, None),
        P("scene", "region", None, None, None),
        P("scene", "region"),
        P("scene", "region"),
        P("scene", None),
        P("scene", None),
    )
    out_specs = (P("scene", "region", None, None, None), P("region", "scene"), P("region", "scene"))
    return jax.shard_map(local, mesh=mesh, in_specs=in_specs, out_specs=out_specs, check_vma=False)
```

time: 686 us -> 106 us (0.15)
  waiting for transfers between devices: 430 us -> 0 us
  local copies, waits for them, and re-layouts: 143 us -> 3.72 us
  Pallas kernels: 0 us -> 97.8 us
  other arithmetic: 46.8 us -> 3.15 us
  matrix products: 23.8 us -> 0 us
  blocking collectives: 20.5 us -> 0 us
  between operations: 16.8 us -> 0.86 us
    all_gather x5 -> x0, waiting for transfers between devices: 202 us -> none  [the longest x1 78.7 us: local(): all_edges = lax.all_gather(edge_rims, 'region', axis=0, tiled=True)]
    psum x1 -> x0, waiting for transfers between devices: 168 us -> none  [local(): full_first, full_second = lax.psum((grad_first, grad_second), 'region')]
    pallas_call x0 -> x3, Pallas kernels: none -> 97.8 us  [the longest x1 50.8 us: reduce(): pl.pallas_call(reduce_kernel, name='reduce', out_shape=jax.ShapeDtypeStru...]
    slice x15 -> x5, local copies, waits for them, and re-layouts: 69.2 us -> 0.05 us  [the longest x1 0.02 us: local(): grad_px = jnp.concatenate([masked[:, 0], masked[:, :, 0]], axis=1)]
    unnamed x10 -> x0, waiting for transfers between devices: 59.6 us -> none
    gather x22 -> x0, local copies, waits for them, and re-layouts: 44.7 us -> none  [fetch(): picked = jnp.take(all_rims, jnp.take(slot_of, position), axis=0)[:, which]]
    dot_general x5 -> x0, matrix products: 23.8 us -> none  [the longest x1 8.03 us: local(): jnp.dot(patches_first, lax.all_gather(w_first, 'scene', axis=0, tiled=Tru...]
    unnamed x1 -> x0, blocking collectives: 20.5 us -> none
  transfers between devices with their start and end apart: 8 -> 0, of which waited for: 7 -> 0; matrix products, arithmetic and copies ran while one was open for 16% -> 0% of each run, Pallas kernels for 0% -> 0%
where the time goes in v1:
time: 106 us; the launch traced here: 105 us
  Pallas kernels  97.8 us (92%)
  local copies, waits for them, and re-layouts  3.72 us (4%)
  other arithmetic  3.15 us (3%)
    pallas_call x1, Pallas kernels, reduce(): pl.pallas_call(reduce_kernel, name='reduce', out_shape=jax.ShapeDtypeStru...  50.8 us
    pallas_call x1, Pallas kernels, exchange(): pl.pallas_call(exchange_kernel, name='exchange', out_shape=(jax.ShapeDtyp...  31.6 us
    pallas_call x1, Pallas kernels, compute(): pl.pallas_call(compute_kernel, name='compute', out_shape=(jax.ShapeDtypeS...  15.4 us

profile of v1, /device:TPU:1, one launch (start us, length us, event | category | flops | bytes accessed | tf_op | source)
XLA Modules:
  0.0 105.5 jit_solution(3463247484789659173)
XLA Ops:
  0.6 0.7 convert_bitcast_fusion.1
  1.3 0.7 convert_bitcast_fusion
  1.9 0.1 broadcast_in_dim.18
  2.0 0.1 broadcast_in_dim.19
  2.1 0.1 broadcast_in_dim.20
  2.2 1.0 bitcast_multiply_fusion.masked
  3.2 0.0 copy-start
  3.3 1.3 %copy.61 = bf16[1,2,32,32,256]{4,3,1,2,0:T(8,128)(2,1)S(1)} copy(bf16[1,2,32,32,256]{4,3,2,1,0:T(8,128)(2,1)} %param.16) | data formatting | bytes 2097152 | tf_op args[0]
  4.8 0.2 concatenate.10
  5.0 0.0 copy-done
  5.0 0.2 fusion.4
  5.3 0.2 copy.62
  5.5 0.8 pad_maximum_fusion.send1
  6.2 31.6 %exchange.1 = (bf16[32,16,256]{2,1,0:T(8,128)(2,1)}, bf16[8,288,256]{2,1,0:T(8,128)(2,1)}, bf16[8,288,256]{2,1,0:T(8,128)(2,1)}) custom-call(bf16[32,16,384]{2,1,0:T(8,128)(2,1)} %pad_maximum_fusion.send1, bf16[288,256]{1,0:T(8,128)(2,1)} %w1.1, bf16[288,256]{1,0:T(8,128)(2,1)} %w2.1), custom_call_target="tpu_custom_call" | custom-call | tf_op jit(solution)/shard_map/exchange/pallas_call | solution.py:214
  37.8 15.4 %compute.1 = (bf16[2,16,16,256]{3,2,1,0:T(8,128)(2,1)}, bf16[4,8,144,256]{3,2,1,0:T(8,128)(2,1)}) custom-call(s32[1,2]{1,0:T(1,128)} %pos.1, bf16[2,32,32,256]{3,2,1,0:T(8,128)(2,1)} %bitcast.54, bf16[2,16,16,256]{3,2,1,0:T(8,128)(2,1)} %copy-done, bf16[32,16,256]{2,1,0:T(8,128)(2,1)} %get-tuple-element.8.halo, bf16[2304,256]{1,0:T(8,128)(2,1)} %bitcast.63, ...), custom_call_target="tpu_custom_call" | custom-call | tf_op jit(solution)/shard_map/compute/pallas_call | solution.py:363
  53.2 50.8 %reduce.1 = f32[32,144]{1,0:T(8,128)} custom-call(bf16[4,8,144,256]{3,2,1,0:T(8,128)(2,1)} %get-tuple-element.12.g), custom_call_target="tpu_custom_call" | custom-call | tf_op jit(solution)/shard_map/reduce/pallas_call | solution.py:481
  104.0 1.5 %slice_bitcast_fusion.4 = (f32[72,32]{0,1:T(8,128)}, f32[72,32]{0,1:T(8,128)}) fusion(f32[32,144]{1,0:T(8,128)} %reduce.1), kind=kLoop, calls=%fused_computation.18 | loop fusion | bytes 36864 | tf_op jit(solution)/shard_map/transpose | solution.py:526
  (20 shorter events, 0.1 us)
Async XLA Ops:
  3.2 1.8 %copy-start = (bf16[2,16,16,256]{3,2,1,0:T(8,128)(2,1)}, bf16[2,16,16,256]{3,2,1,0:T(8,128)(2,1)S(1)}, u32[]{:S(2)}) copy-start(bf16[2,16,16,256]{3,2,1,0:T(8,128)(2,1)S(1)} %bitcast_multiply_fusion.masked) | copy-start | bytes 786436

commit v2 on v0

v2 whole, which is shorter than its diff:
```python
import math

import jax
import jax.numpy as jnp
import ml_dtypes
import numpy as np
from jax import lax
from jax.experimental import pallas as pl
from jax.experimental.pallas import tpu as pltpu
from jax.sharding import PartitionSpec as P

MESH = pl.DeviceIdType.MESH
BF = jnp.bfloat16
F32 = jnp.float32
GW, GH = 4, 16
C = 256
REG, ZN, YN, SC = 32, 8, 4, 8
WROWS = 288
LEFT = 48
ROWS = 9 * C
OWN_ROWS = ROWS // REG
VMEM_LIMIT = 56 * 1024 * 1024


def hot(rows, cols, pairs):
    out = np.zeros((rows, cols), np.float32)
    for row, col in pairs:
        out[row, col] = 1.0
    return out.astype(ml_dtypes.bfloat16)


def place_tables():
    tile = lambda h, w: 32 * h + w
    corner = ((30, 30), (30, 31), (31, 30), (31, 31), (30, 0), (31, 0), (0, 30), (0, 31), (0, 0))
    rim = hot(256, 1024, [
        (8 * k + q, px) for k in range(32) for q, px in enumerate((
            tile(31, k), tile(30, k), tile(k, 31), tile(k, 30), tile(0, k), tile(k, 0)))
    ] + [(8 * k + 7, tile(*at)) for k, at in enumerate(corner)])
    rim_grad = hot(256, 256, [(8 * k + 6, k if k < 16 else 16 * (k - 16)) for k in range(32)] + [(79, 0)])

    cols = lambda blk, b: 2 * b - 1 + blk
    order = (1, 2, 0, 3)
    body = hot(512, 256, [
        (at * 128 + h * 16 + b, h * 32 + cols(blk, b))
        for at, blk in enumerate(order) for h in range(8) for b in range(16) if 0 <= cols(blk, b) < 32
    ])
    sides = hot(256, 64, [(h * 16, 8 * h + 2) for h in range(8)]
                + [(128 + h * 16 + 15, 8 * h + 5) for h in range(8)])
    edge_q = (1, 0, 4)
    corner_left, corner_right = (1, 3, 7), (4, 5, 8)

    def edge_source(sel, col):
        if col < 0:
            return 8 * corner_left[sel] + 7
        if col > 31:
            return 8 * corner_right[sel] + 7
        return 8 * col + edge_q[sel]

    edges = hot(192, 256, [
        (sel * 64 + blk * 16 + b, edge_source(sel, cols(blk, b)))
        for sel in range(3) for blk in range(4) for b in range(16)
    ])

    def left_source(hh, j):
        if 0 <= hh < 32:
            return 8 * hh + (3, 2)[j] if j < 2 else None
        sel = {-2: 0, -1: 1, 32: 2}[hh]
        if j < 2:
            return 8 * ((0, 1), (2, 3), (6, 7))[sel][j] + 7
        return edge_q[sel]

    left = hot(9 * LEFT, 256, [
        ((3 * i + j) * LEFT + g, left_source(g + i - 2, j))
        for i in range(3) for j in range(3) for g in range(33)
        if left_source(g + i - 2, j) is not None
    ])
    first_col = hot(3 * LEFT, 256, [
        (i * LEFT + g, 8 * (g + i - 2) + 5) for i in range(3) for g in range(33) if 0 <= g + i - 2 < 32
    ])
    shift = hot(272, 272, [(a * 16 + b, a * 16 + b - 1) for a in range(17) for b in range(1, 16)])
    from_left = np.stack([
        hot(272, LEFT, [(a * 16, 2 * a + par) for a in range(17 - par)]) for par in range(2)
    ])
    back = hot(272, 256, [(a * 16 + b, a * 16 + b + 1) for a in range(16) for b in range(15)])
    below = hot(16, 256, [(b, 8 * b + 6) for b in range(16)])
    beside = hot(272, 256, [(a * 16 + 15, 8 * (16 + a) + 6) for a in range(16)]
                 + [(256 + b, 8 * (b + 1) + 6) for b in range(15)] + [(271, 79)])
    return rim, rim_grad, body, sides, edges, left, first_col, shift, from_left, back, below, beside


def dot(a, b):
    return jnp.dot(a, b, preferred_element_type=F32)


def dot_t(a, b):
    return lax.dot_general(a, b, (((1,), (1,)), ((), ())), preferred_element_type=F32)


def sigmoid(v):
    return 1.0 / (1.0 + jnp.exp(-v))


def route_rows(pos, r):
    lane = lax.broadcasted_iota(jnp.int32, (512, 128), 1).astype(F32)
    q = lax.broadcasted_iota(jnp.int32, (512, 128), 0) % 8
    zero = jnp.zeros((512, 128), F32)
    k = zero.astype(jnp.int32) + r
    grad_row = jnp.where(k < 16, 1.0, 0.0)
    corner_row = jnp.where(k < 6, -1.0, 1.0)
    corner_col = jnp.where((k < 4) | (k == 6) | (k == 7), -1.0, 1.0)
    d_row = jnp.where(q < 2, -1.0, jnp.where(q == 4, 1.0, zero))
    d_row = jnp.where(q == 6, grad_row, jnp.where(q == 7, corner_row, d_row))
    d_col = jnp.where((q == 2) | (q == 3), -1.0, jnp.where(q == 5, 1.0, zero))
    d_col = jnp.where(q == 6, 1.0 - grad_row, jnp.where(q == 7, corner_col, d_col))
    p_row = jnp.floor(pos * 0.25)
    n_row = p_row + d_row
    n_col = pos - 4.0 * p_row + d_col
    inside = (n_row >= 0.0) & (n_row < GH) & (n_col >= 0.0) & (n_col < GW)
    want = jnp.where(inside, 4.0 * n_row + n_col, -1.0)
    has = jnp.where(pos == lane, 1.0, 0.0).astype(BF)
    wants = jnp.where(want == lane, 1.0, 0.0).astype(BF)
    same = (lax.broadcasted_iota(jnp.int32, (512, 512), 0) % 8) == (
        lax.broadcasted_iota(jnp.int32, (512, 512), 1) % 8)
    return jnp.where(same, dot_t(wants, has), 0.0).astype(BF)


Z_ORDER = (4, 3, 5, 2, 6, 1, 7, 0)


def level_kernel(positions, clear, tiles, cotangent, w1_here, w2_here, *refs):
    names = list(TABLES)
    table_hbm = dict(zip(names, refs[:len(names)]))
    feat, out = refs[len(names):len(names) + 2]
    refs = refs[len(names) + 2:]
    table = dict(zip(names, refs[:len(names)]))
    (table_sem, pos_send, pos_buf, send1, recv1, send2, recv2, masked, own_rim, halo, w1, w2,
     x4, h_odd, h_even, left_x, slopes, grad_t, g_f, g, f_buf, o_buf, s_buf, s_send, z_send, z_buf,
     n_send, n_buf, x_send, x_buf, c_send, c_buf,
     a2a_s, a2a_r, w_s, w_r, v_s, v_r, y_s, y_r, zs, zr, xs, xr, cs, cr, own_sem) = refs[len(names):]

    s = lax.axis_index("scene")
    r = lax.axis_index("region")
    z, y = r // YN, r % YN
    sib = s + 1 - 2 * (s % 2)

    loads = {name: pltpu.make_async_copy(table_hbm[name], table[name], table_sem.at[n])
             for n, name in enumerate(names)}
    for name in names:
        loads[name].start()

    barrier = pltpu.get_barrier_semaphore()

    def greet(o, carry):
        pl.semaphore_signal(barrier, inc=1, device_id={"region": (r + o) % REG}, device_id_type=MESH)
        return carry

    lax.fori_loop(1, REG, greet, 0)
    for o in range(1, SC):
        pl.semaphore_signal(barrier, inc=1, device_id={"scene": (s + o) % SC}, device_id_type=MESH)

    def w_rows(ref, who):
        return ref.at[pl.ds(pl.multiple_of(who * WROWS, 32), WROWS)]

    weights = ((w1_here, w1), (w2_here, w2))
    own = [pltpu.make_async_copy(src, w_rows(dst, s), own_sem.at[n]) for n, (src, dst) in enumerate(weights)]
    for copy in own:
        copy.start()

    def all_to_all(n, src, dst):
        def send(o, carry):
            to = (r + o) % REG
            pltpu.make_async_remote_copy(
                src_ref=src(to), dst_ref=dst(r), send_sem=a2a_s.at[n], recv_sem=a2a_r.at[n],
                device_id={"region": to}, device_id_type=MESH).start()
            return carry

        lax.fori_loop(1, REG, send, 0)

    def await_all(buf, sem):
        pltpu.make_async_copy(buf, buf, sem).wait()

    own_pos = [positions[0:1, t:t + 1].astype(F32) for t in range(2)]
    for t in range(2):
        pos_send[t] = jnp.broadcast_to(own_pos[t], (1, 128))
        kept = clear[0:1, t:t + 1].astype(F32)
        masked[t] = (cotangent[t].reshape(256, C).astype(F32) * kept).astype(BF)
    pl.semaphore_wait(barrier, REG - 1 + SC - 1)

    right, left_chip = (s + 2) % SC, (s + 6) % SC

    def to_scene(src, dst, send_sem, recv_sem, who):
        copy = pltpu.make_async_remote_copy(
            src_ref=src, dst_ref=dst, send_sem=send_sem, recv_sem=recv_sem,
            device_id={"scene": who}, device_id_type=MESH)
        copy.start()
        return copy

    all_to_all(0, lambda to: pos_send, lambda me: pos_buf.at[pl.ds(2 * me, 2)])
    far, near = [], []
    for n, (src, dst) in enumerate(weights):
        far.append(to_scene(src, w_rows(dst, s), w_s.at[n, 0], w_r.at[n, 0], right))
        far.append(to_scene(src, w_rows(dst, s), w_s.at[n, 1], w_r.at[n, 1], left_chip))
        near.append([to_scene(src, w_rows(dst, s), v_s.at[n, 0], v_r.at[n, 0], sib)])

    loads["rim"].wait()
    loads["rim_grad"].wait()
    rims = []
    for t in range(2):
        rim = dot(table["rim"][...], tiles[t].reshape(1024, C)) + dot(table["rim_grad"][...], masked[t])
        own_rim[t] = rim.astype(BF)
        rims.append(rim.reshape(REG, 8, C))
    send1[...] = jnp.concatenate(rims, axis=1).astype(BF)
    all_to_all(1, lambda to: send1.at[to], lambda me: recv1.at[me])
    recv1[r] = send1[r]
    for t in range(2):
        pos_buf[2 * r + t] = pos_send[t]

    loads["body"].wait()
    for t in range(2):
        for c in range(4):
            chunk = tiles[t, 8 * c:8 * c + 8].reshape(256, C)
            got = dot(table["body"][:256], chunk).astype(BF)
            for at, blk in enumerate((1, 2)):
                x4[t, 4 * c + 1:4 * c + 5, :, :, blk * C:(blk + 1) * C] = (
                    got[at * 128:(at + 1) * 128].reshape(4, 2, 16, C))

    await_all(pos_buf.at[pl.ds(0, 2 * REG - 2)], a2a_r.at[0])
    route = route_rows(jnp.broadcast_to(pos_buf[...], (64, 8, 128)).reshape(512, 128), r)

    def forward(n, came, at):
        rows = w_rows(weights[n][1], came)
        return to_scene(rows, rows, v_s.at[n, at], v_r.at[n, at], sib)

    far[0].wait_recv()
    rows = w_rows(w1, left_chip)
    far.append(to_scene(rows, rows, w_s.at[0, 2], w_r.at[0, 2], right))
    near[0].append(forward(0, left_chip, 1))
    far[1].wait_recv()
    near[0].append(forward(0, right, 2))

    await_all(recv1.at[pl.ds(0, REG - 1)], a2a_r.at[1])
    send2[...] = dot(route, recv1[...].reshape(512, C)).astype(BF).reshape(REG, 16, C)
    all_to_all(2, lambda to: send2.at[to], lambda me: recv2.at[me])
    recv2[r] = send2[r]

    far[2].wait_recv()
    near[1].append(forward(1, left_chip, 1))
    far[3].wait_recv()
    rows = w_rows(w2, right)
    far.append(to_scene(rows, rows, w_s.at[1, 2], w_r.at[1, 2], left_chip))
    near[1].append(forward(1, right, 2))
    opposite = (s + 4) % SC
    far[4].wait_recv()
    near[0].append(forward(0, opposite, 3))

    m_t = jnp.concatenate([masked[t].astype(F32).T.astype(BF) for t in range(2)], axis=1)
    for name in names[3:]:
        loads[name].wait()
    far[5].wait_recv()
    near[1].append(forward(1, opposite, 3))
    await_all(recv2.at[pl.ds(0, REG - 1)], a2a_r.at[2])

    came = recv2[...].astype(F32)
    for t in range(2):
        halo[t] = came[:, 8 * t:8 * t + 8].reshape(256, C).astype(BF)
    for t in range(2):
        for c in range(4):
            chunk = tiles[t, 8 * c:8 * c + 8].reshape(256, C)
            got = dot(table["body"][256:], chunk) + dot(table["sides"][...], halo[t, 64 * c:64 * c + 64])
            got = got.astype(BF)
            for at, blk in enumerate((0, 3)):
                x4[t, 4 * c + 1:4 * c + 5, :, :, blk * C:(blk + 1) * C] = (
                    got[at * 128:(at + 1) * 128].reshape(4, 2, 16, C))
        rim = dot(table["edges"][...], halo[t]).astype(BF)
        for sel, (pair, par) in enumerate(((0, 0), (0, 1), (17, 0))):
            for blk in range(4):
                start = sel * 64 + blk * 16
                x4[t, pair, par, :, blk * C:(blk + 1) * C] = rim[start:start + 16]
        side = dot(table["left"][...], halo[t])
        inner = dot(table["first_col"][...], own_rim[t])
        for i in range(3):
            for j in range(3):
                tap = 3 * i + j
                part = side[tap * LEFT:(tap + 1) * LEFT]
                if j == 2:
                    part = part + inner[i * LEFT:(i + 1) * LEFT]
                left_x[t * LEFT:(t + 1) * LEFT, tap * C:(tap + 1) * C] = part.astype(BF)

    own[0].wait()
    for copy in near[0]:
        copy.wait_recv()

    pre_left = dot(left_x[...], w1[...])
    row_id = lax.broadcasted_iota(jnp.int32, (LEFT, C), 0)
    hidden_left, above = [], []
    for t in range(2):
        p_row = jnp.floor(own_pos[t] * 0.25)
        has_left = jnp.where(own_pos[t] - 4.0 * p_row > 0.0, 1.0, 0.0)
        has_above = jnp.where(p_row > 0.0, 1.0, 0.0)
        above.append(has_above)
        v = pre_left[t * LEFT:(t + 1) * LEFT]
        keep = jnp.where(row_id == 0, has_left * has_above, has_left)
        hidden_left.append((v * sigmoid(v) * keep).astype(BF))

    def window(t, par, i, cp):
        row = par + i
        n = 17 - par
        return x4[t, row // 2:row // 2 + n, row % 2, :, cp * C:cp * C + 768].reshape(n * 16, 768)

    for t in range(2):
        for par in range(2):
            store = h_odd if par == 0 else h_even
            n = 17 - par
            for cp in range(2):
                patch = jnp.concatenate([window(t, par, i, cp) for i in range(3)], axis=1)
                pre = dot(patch, w1[...])
                sig = sigmoid(pre)
                act = pre * sig
                if par == 0:
                    own_row = lax.broadcasted_iota(jnp.int32, (272, C), 0) >= 16
                    act = jnp.where(own_row, act, act * above[t])
                act = act.astype(BF)
                if cp == 0:
                    store[t, :, :, C:2 * C] = act.reshape(n, 16, C)
                else:
                    store[t, :, :, 2 * C:] = act.reshape(n, 16, C)
                    moved = dot(table["shift"][:n * 16, :n * 16], act)
                    moved = moved + dot(table["from_left"][par, :n * 16], hidden_left[t])
                    store[t, :, :, :C] = moved.astype(BF).reshape(n, 16, C)
                if par == 0:
                    pre, sig = pre[16:], sig[16:]
                slopes[4 * t + 2 * par + cp] = sig * (1.0 + pre * (1.0 - sig))

    def hidden_rows(t, i):
        if i == 1:
            return h_even[t].reshape(256, 768)
        return h_odd[t, i // 2:i // 2 + 16].reshape(256, 768)

    def blocks(n):
        for yy in range(YN):
            for zz in range(ZN):
                start = OWN_ROWS * (zz * YN + yy)
                rows = g_f[start:start + OWN_ROWS, :]
                g[n, yy, zz] = jnp.concatenate([rows[:, :128], rows[:, 128:]], axis=0).astype(BF)

    def to_region(src, dst, send_sem, recv_sem, who):
        copy = pltpu.make_async_remote_copy(
            src_ref=src, dst_ref=dst, send_sem=send_sem, recv_sem=recv_sem,
            device_id={"region": who}, device_id_type=MESH)
        copy.start()
        return copy

    sent = []
    y_copies = {}

    def turn(oz):
        return 1 if oz % 2 == 0 else YN - 1

    def y_first(n):
        for kind in range(2):
            for oz in Z_ORDER:
                d = turn(oz)
                block = (y + 2) % YN if kind == 0 else (y + YN - d) % YN
                who = (y + d) % YN if kind == 0 else block
                buf = f_buf if kind == 0 else o_buf
                y_copies[n, kind, oz] = to_region(
                    g.at[n, block, (z + oz) % ZN], buf.at[n, oz],
                    y_s.at[kind, n, oz], y_r.at[kind, n, oz], z * YN + who)
                sent.append(y_copies[n, kind, oz])

    def y_second(n):
        for oz in Z_ORDER:
            who = (y + turn(oz)) % YN
            y_copies[n, 0, oz].wait_recv()
            summed = g[n, who, (z + oz) % ZN].astype(F32) + f_buf[n, oz].astype(F32)
            s_send[n, oz] = summed.astype(BF)
            y_copies[n, 2, oz] = to_region(
                s_send.at[n, oz], s_buf.at[n, oz], y_s.at[2, n, oz], y_r.at[2, n, oz], z * YN + who)
            sent.append(y_copies[n, 2, oz])

    def z_first(n):
        copies = []
        for oz in Z_ORDER:
            y_copies[n, 1, oz].wait_recv()
            y_copies[n, 2, oz].wait_recv()
            total = (g[n, y, (z + oz) % ZN].astype(F32) + o_buf[n, oz].astype(F32)) + s_buf[n, oz].astype(F32)
            if oz:
                z_send[n, oz - 1] = total.astype(BF)
                copies.append(to_region(
                    z_send.at[n, oz - 1], z_buf.at[n, oz - 1], zs.at[n, oz - 1], zr.at[n, oz - 1],
                    ((z + oz) % ZN) * YN + y))
        sent.extend(copies)
        return total, copies

    def z_second(n, total, copies):
        for at, copy in enumerate(copies):
            copy.wait_recv()
            total = total + z_buf[n, Z_ORDER[at] - 1].astype(F32)
        return total

    for i in range(3):
        for j in range(3):
            tap = 3 * i + j
            seen = jnp.concatenate([hidden_rows(t, i)[:, j * C:(j + 1) * C] for t in range(2)], axis=0)
            g_f[tap * C:(tap + 1) * C, :] = dot(m_t, seen).T
    blocks(1)
    y_first(1)

    own[1].wait()
    for copy in near[1]:
        copy.wait_recv()
    for t in range(2):
        patch = jnp.concatenate([hidden_rows(t, i) for i in range(3)], axis=1)
        feat[t] = dot(patch, w2[...]).astype(BF).reshape(16, 16, C)

    def second(tap):
        return w2[tap * C:(tap + 1) * C, :]

    up, down = slice(0, 256), slice(16, 272)
    for t in range(2):
        if t == 1:
            y_second(1)
        m0 = jnp.concatenate([masked[t], dot(table["below"][...], halo[t]).astype(BF)], axis=0)
        m1 = (dot(table["back"][...], masked[t]) + dot(table["beside"][...], halo[t])).astype(BF)
        spread = (
            dot_t(m0[up], second(7)) + dot_t(m0[down], second(1)),
            (dot_t(m0[up], second(8)) + dot_t(m1[up], second(6))
             + dot_t(m0[down], second(2)) + dot_t(m1[down], second(0))),
            dot_t(m0[up], second(4)),
            dot_t(m0[up], second(5)) + dot_t(m1[up], second(3)),
        )
        for n in range(4):
            group = 4 * t + n
            grad_t[:, group * 256:(group + 1) * 256] = (spread[n] * slopes[group]).T.astype(BF)

    def own_rows(t, par, i, cp, j):
        row = (2 if par == 0 else 1) + i
        lanes = (cp + j) * C
        return x4[t, row // 2:row // 2 + 16, row % 2, :, lanes:lanes + C].reshape(256, C)

    for i in range(3):
        if i == 2:
            z_second_left = z_first(1)
        for j in range(3):
            tap = 3 * i + j
            seen = jnp.concatenate(
                [own_rows(t, par, i, cp, j) for t in range(2) for par in range(2) for cp in range(2)], axis=0)
            g_f[tap * C:(tap + 1) * C, :] = dot(grad_t[...], seen).T
    blocks(0)
    y_first(0)
    y_second(0)
    total_second = z_second(1, *z_second_left)
    total_first = z_second(0, *z_first(0))

    squares = jnp.sum(total_first * total_first + total_second * total_second, axis=0, keepdims=True)
    n_send[0] = squares
    all_to_all(3, lambda to: n_send.at[0], lambda me: n_buf.at[me])
    n_buf[r] = squares
    for n, total in enumerate((total_first, total_second)):
        turned = jnp.concatenate([total[:OWN_ROWS].T, total[OWN_ROWS:].T], axis=0)
        x_send[:, n] = turned.reshape(SC, 32, OWN_ROWS)
    x_copies = []
    for o in range(1, SC):
        to = (s + o) % SC
        x_copies.append(to_scene(x_send.at[to], x_buf.at[o - 1], xs.at[o - 1], xr.at[o - 1], to))
    await_all(n_buf.at[pl.ds(0, REG - 1)], a2a_r.at[3])
    sum_sq = jnp.sum(n_buf[...].reshape(REG, 128), keepdims=True)
    factor = (3.0 * C * math.sqrt(2.0) / SC) / (jnp.sqrt(sum_sq) + 0.01)
    c_send[0] = jnp.broadcast_to(factor, (1, 128))
    c_copies = []
    for o in range(1, SC):
        to = (s + o) % SC
        c_copies.append(to_scene(c_send.at[0], c_buf.at[o - 1], cs.at[o - 1], cr.at[o - 1], to))
    result = x_send[s] * factor.reshape(1, 1, 1)
    for o in range(1, SC):
        x_copies[o - 1].wait_recv()
        c_copies[o - 1].wait_recv()
        result = result + x_buf[o - 1] * c_buf[o - 1][:, :1].reshape(1, 1, 1)
    out[...] = result

    for copy in far + near[0] + near[1] + sent + x_copies + c_copies:
        copy.wait_send()
    await_all(pos_buf.at[pl.ds(0, 2 * REG - 2)], a2a_s.at[0])
    await_all(send1.at[pl.ds(0, REG - 1)], a2a_s.at[1])
    await_all(send2.at[pl.ds(0, REG - 1)], a2a_s.at[2])
    await_all(n_buf.at[pl.ds(0, REG - 1)], a2a_s.at[3])


NAMES = ("rim", "rim_grad", "body", "sides", "edges", "left", "first_col", "shift", "from_left",
         "back", "below", "beside")
TABLES = dict(zip(NAMES, place_tables()))


def level(positions, clear, tiles, cotangent, w1, w2):
    vmem = pl.BlockSpec(memory_space=pltpu.VMEM)
    anywhere = pl.BlockSpec(memory_space=pl.ANY)
    dma = pltpu.SemaphoreType.DMA
    tables = list(TABLES.values())
    part = (144, 128)
    return pl.pallas_call(
        level_kernel,
        name="level",
        out_shape=(jax.ShapeDtypeStruct((2, 16, 16, C), BF), jax.ShapeDtypeStruct((2, 32, OWN_ROWS), F32)),
        in_specs=[vmem] * 4 + [anywhere] * (2 + len(tables)),
        out_specs=(vmem, vmem),
        scratch_shapes=[pltpu.VMEM(t.shape, BF) for t in tables] + [
            dma((len(tables),)),
            pltpu.VMEM((2, 1, 128), F32), pltpu.VMEM((2 * REG, 1, 128), F32),
            pltpu.VMEM((REG, 16, C), BF), pltpu.VMEM((REG, 16, C), BF),
            pltpu.VMEM((REG, 16, C), BF), pltpu.VMEM((REG, 16, C), BF),
            pltpu.VMEM((2, 256, C), BF), pltpu.VMEM((2, 256, C), BF), pltpu.VMEM((2, 256, C), BF),
            pltpu.VMEM((ROWS, C), BF), pltpu.VMEM((ROWS, C), BF),
            pltpu.VMEM((2, 18, 2, 16, 4 * C), BF),
            pltpu.VMEM((2, 17, 16, 3 * C), BF), pltpu.VMEM((2, 16, 16, 3 * C), BF),
            pltpu.VMEM((2 * LEFT, ROWS), BF),
            pltpu.VMEM((8, 256, C), F32),
            pltpu.VMEM((C, 2048), BF),
            pltpu.VMEM((ROWS, C), F32),
            pltpu.VMEM((2, YN, ZN) + part, BF),
            pltpu.VMEM((2, ZN) + part, BF), pltpu.VMEM((2, ZN) + part, BF),
            pltpu.VMEM((2, ZN) + part, BF), pltpu.VMEM((2, ZN) + part, BF),
            pltpu.VMEM((2, ZN - 1) + part, BF), pltpu.VMEM((2, ZN - 1) + part, BF),
            pltpu.VMEM((1, 1, 128), F32), pltpu.VMEM((REG, 1, 128), F32),
            pltpu.VMEM((SC, 2, 32, OWN_ROWS), F32), pltpu.VMEM((SC - 1, 2, 32, OWN_ROWS), F32),
            pltpu.VMEM((1, 1, 128), F32), pltpu.VMEM((SC - 1, 1, 128), F32),
            dma((4,)), dma((4,)), dma((2, 3)), dma((2, 3)), dma((2, 4)), dma((2, 4)),
            dma((3, 2, ZN)), dma((3, 2, ZN)), dma((2, ZN - 1)), dma((2, ZN - 1)),
            dma((SC - 1,)), dma((SC - 1,)), dma((SC - 1,)), dma((SC - 1,)), dma((2,)),
        ],
        compiler_params=pltpu.CompilerParams(
            collective_id=0, has_side_effects=True, vmem_limit_bytes=VMEM_LIMIT),
    )(positions, clear, tiles, cotangent, w1, w2, *[jnp.asarray(t) for t in tables])


def local(tiles, cotangent, positions, clear, w_first, w_second):
    feat, out = level(positions, clear, tiles[0], cotangent[0], w_first, w_second)
    return feat[None], out[0].T, out[1].T


def solution(mesh):
    in_specs = (
        P("scene", "region", None, None, None),
        P("scene", "region", None, None, None),
        P("scene", "region"),
        P("scene", "region"),
        P("scene", None),
        P("scene", None),
    )
    out_specs = (P("scene", "region", None, None, None), P("region", "scene"), P("region", "scene"))
    return jax.shard_map(local, mesh=mesh, in_specs=in_specs, out_specs=out_specs, check_vma=False)
```

time: 686 us -> 81.4 us (0.12)
  waiting for transfers between devices: 430 us -> 0 us
  local copies, waits for them, and re-layouts: 143 us -> 3.02 us
  Pallas kernels: 0 us -> 77.5 us
  other arithmetic: 46.8 us -> 0 us
  matrix products: 23.8 us -> 0 us
  blocking collectives: 20.5 us -> 0 us
  between operations: 16.8 us -> 0.64 us
    all_gather x5 -> x0, waiting for transfers between devices: 202 us -> none  [the longest x1 78.7 us: local(): all_edges = lax.all_gather(edge_rims, 'region', axis=0, tiled=True)]
    psum x1 -> x0, waiting for transfers between devices: 168 us -> none  [local(): full_first, full_second = lax.psum((grad_first, grad_second), 'region')]
    pallas_call x0 -> x1, Pallas kernels: none -> 77.5 us  [level(): pl.pallas_call(level_kernel, name='level', out_shape=(jax.ShapeDtypeStruc...]
    slice x16 -> x0, local copies, waits for them, and re-layouts: 70.4 us -> none  [the longest x9 67.2 us: tap_patches(): padded[:, tap_row:tap_row + stride * out_side:stride, tap_col:tap_col + s...]
    unnamed x10 -> x0, waiting for transfers between devices: 59.6 us -> none
    gather x22 -> x0, local copies, waits for them, and re-layouts: 44.7 us -> none  [fetch(): picked = jnp.take(all_rims, jnp.take(slot_of, position), axis=0)[:, which]]
    dot_general x5 -> x0, matrix products: 23.8 us -> none  [the longest x1 8.03 us: local(): jnp.dot(patches_first, lax.all_gather(w_first, 'scene', axis=0, tiled=Tru...]
    unnamed x1 -> x0, blocking collectives: 20.5 us -> none
  transfers between devices with their start and end apart: 8 -> 0, of which waited for: 7 -> 0; matrix products, arithmetic and copies ran while one was open for 16% -> 0% of each run, Pallas kernels for 0% -> 0%
where the time goes in v2:
time: 81.4 us; the launch traced here: 81.1 us
  Pallas kernels  77.5 us (95%)
  local copies, waits for them, and re-layouts  3.02 us (4%)
    pallas_call x1, Pallas kernels, level(): pl.pallas_call(level_kernel, name='level', out_shape=(jax.ShapeDtypeStruc...  77.5 us
    unnamed x1, local copies, waits for them, and re-layouts  1.67 us

profile of v2, /device:TPU:1, one launch (start us, length us, event | category | flops | bytes accessed | tf_op | source)
XLA Modules:
  0.0 81.1 jit_solution(12031003206354519112)
XLA Ops:
  0.6 77.5 %level.1 = (bf16[2,16,16,256]{3,2,1,0:T(8,128)(2,1)}, f32[2,32,72]{2,1,0:T(8,128)}) custom-call(s32[1,2]{1,0:T(1,128)} %positions.1, s32[1,2]{1,0:T(1,128)} %clear.1, bf16[2,32,32,256]{3,2,1,0:T(8,128)(2,1)} %bitcast.11, bf16[2,16,16,256]{3,2,1,0:T(8,128)(2,1)} %bitcast.12, bf16[288,256]{1,0:T(8,128)(2,1)} %w1_here.1, bf16[288,256]{1,0:T(8,128)(2,1)} %w2_here.1, ...), custom_call_target="tpu_custom_call" | custom-call | tf_op jit(solution)/shard_map/level/pallas_call | solution.py:500
  78.1 1.3 %slice_bitcast_fusion = (f32[72,32]{0,1:T(8,128)}, f32[72,32]{0,1:T(8,128)}) fusion(f32[2,32,72]{2,1,0:T(8,128)} %get-tuple-element.6), kind=kLoop, calls=%fused_computation | loop fusion | bytes 36864 | tf_op jit(solution)/shard_map/transpose | solution.py:537
  79.5 1.7 %copy.22 = bf16[1,2,16,16,256]{4,3,2,1,0:T(8,128)(2,1)} copy(bf16[1,2,16,16,256]{4,3,2,1,0:T(8,128)(2,1)} %bitcast.13) | data formatting | bytes 524288

commit v3 on v2

--- a/solution.py
+++ b/solution.py
@@ -96,8 +96,12 @@
     return lax.dot_general(a, b, (((1,), (1,)), ((), ())), preferred_element_type=F32)
 
 
+def dot_l(a, b):
+    return lax.dot_general(a, b, (((0,), (0,)), ((), ())), preferred_element_type=F32)
+
+
 def sigmoid(v):
-    return 1.0 / (1.0 + jnp.exp(-v))
+    return 0.5 * jnp.tanh(0.5 * v) + 0.5
 
 
 def route_rows(pos, r):
@@ -127,14 +131,14 @@
 Z_ORDER = (4, 3, 5, 2, 6, 1, 7, 0)
 
 
-def level_kernel(positions, clear, tiles, cotangent, w1_here, w2_here, *refs):
+def level_kernel(positions_hbm, clear_hbm, tiles_hbm, cotangent_hbm, w1_here, w2_here, *refs):
     names = list(TABLES)
     table_hbm = dict(zip(names, refs[:len(names)]))
     feat, out = refs[len(names):len(names) + 2]
     refs = refs[len(names) + 2:]
     table = dict(zip(names, refs[:len(names)]))
-    (table_sem, pos_send, pos_buf, send1, recv1, send2, recv2, masked, own_rim, halo, w1, w2,
-     x4, h_odd, h_even, left_x, slopes, grad_t, g_f, g, f_buf, o_buf, s_buf, s_send, z_send, z_buf,
+    (positions, clear, tiles, cotangent, in_sem, table_sem, pos_send, pos_buf, send1, recv1, send2, recv2, masked, own_rim, halo, w1, w2,
+     x4, h_odd, h_even, left_x, slopes, d_pre, g_f, g, f_buf, o_buf, s_buf, s_send, z_send, z_buf,
      n_send, n_buf, x_send, x_buf, c_send, c_buf,
      a2a_s, a2a_r, w_s, w_r, v_s, v_r, y_s, y_r, zs, zr, xs, xr, cs, cr, own_sem) = refs[len(names):]
 
@@ -143,6 +147,10 @@
     z, y = r // YN, r % YN
     sib = s + 1 - 2 * (s % 2)
 
+    arrays = [pltpu.make_async_copy(src, dst, in_sem.at[n]) for n, (src, dst) in enumerate((
+        (positions_hbm, positions), (clear_hbm, clear), (tiles_hbm, tiles), (cotangent_hbm, cotangent)))]
+    for copy in arrays:
+        copy.start()
     loads = {name: pltpu.make_async_copy(table_hbm[name], table[name], table_sem.at[n])
              for n, name in enumerate(names)}
     for name in names:
@@ -168,22 +176,25 @@
 
     def all_to_all(n, src, dst):
         def send(o, carry):
-            to = (r + o) % REG
+            step, turn_y = o // YN, o % YN
+            dz = ZN // 2 + ((step + 1) // 2) * (1 - 2 * (step % 2))
+            dy = YN // 2 + ((turn_y + 1) // 2) * (1 - 2 * (turn_y % 2))
+            to = ((z + dz) % ZN) * YN + (y + dy) % YN
             pltpu.make_async_remote_copy(
                 src_ref=src(to), dst_ref=dst(r), send_sem=a2a_s.at[n], recv_sem=a2a_r.at[n],
                 device_id={"region": to}, device_id_type=MESH).start()
             return carry
 
-        lax.fori_loop(1, REG, send, 0)
+        lax.fori_loop(0, REG - 1, send, 0)
 
     def await_all(buf, sem):
         pltpu.make_async_copy(buf, buf, sem).wait()
 
+    for copy in arrays[:2]:
+        copy.wait()
     own_pos = [positions[0:1, t:t + 1].astype(F32) for t in range(2)]
     for t in range(2):
         pos_send[t] = jnp.broadcast_to(own_pos[t], (1, 128))
-        kept = clear[0:1, t:t + 1].astype(F32)
-        masked[t] = (cotangent[t].reshape(256, C).astype(F32) * kept).astype(BF)
     pl.semaphore_wait(barrier, REG - 1 + SC - 1)
 
     right, left_chip = (s + 2) % SC, (s + 6) % SC
@@ -197,11 +208,20 @@
 
     all_to_all(0, lambda to: pos_send, lambda me: pos_buf.at[pl.ds(2 * me, 2)])
     far, near = [], []
-    for n, (src, dst) in enumerate(weights):
+
+    def send_weights(n):
+        src, dst = weights[n]
         far.append(to_scene(src, w_rows(dst, s), w_s.at[n, 0], w_r.at[n, 0], right))
         far.append(to_scene(src, w_rows(dst, s), w_s.at[n, 1], w_r.at[n, 1], left_chip))
         near.append([to_scene(src, w_rows(dst, s), v_s.at[n, 0], v_r.at[n, 0], sib)])
 
+    send_weights(0)
+
+    for copy in arrays[2:]:
+        copy.wait()
+    for t in range(2):
+        kept = clear[0:1, t:t + 1].astype(F32)
+        masked[t] = (cotangent[t].reshape(256, C).astype(F32) * kept).astype(BF)
     loads["rim"].wait()
     loads["rim_grad"].wait()
     rims = []
@@ -224,40 +244,35 @@
                 x4[t, 4 * c + 1:4 * c + 5, :, :, blk * C:(blk + 1) * C] = (
                     got[at * 128:(at + 1) * 128].reshape(4, 2, 16, C))
 
-    await_all(pos_buf.at[pl.ds(0, 2 * REG - 2)], a2a_r.at[0])
-    route = route_rows(jnp.broadcast_to(pos_buf[...], (64, 8, 128)).reshape(512, 128), r)
-
     def forward(n, came, at):
         rows = w_rows(weights[n][1], came)
         return to_scene(rows, rows, v_s.at[n, at], v_r.at[n, at], sib)
 
+    opposite = (s + 4) % SC
     far[0].wait_recv()
     rows = w_rows(w1, left_chip)
     far.append(to_scene(rows, rows, w_s.at[0, 2], w_r.at[0, 2], right))
     near[0].append(forward(0, left_chip, 1))
     far[1].wait_recv()
     near[0].append(forward(0, right, 2))
-
+    send_weights(1)
+    await_all(pos_buf.at[pl.ds(0, 2 * REG - 2)], a2a_r.at[0])
+    route = route_rows(jnp.broadcast_to(pos_buf[...], (64, 8, 128)).reshape(512, 128), r)
     await_all(recv1.at[pl.ds(0, REG - 1)], a2a_r.at[1])
     send2[...] = dot(route, recv1[...].reshape(512, C)).astype(BF).reshape(REG, 16, C)
     all_to_all(2, lambda to: send2.at[to], lambda me: recv2.at[me])
     recv2[r] = send2[r]
 
+    for name in names[3:]:
+        loads[name].wait()
     far[2].wait_recv()
+    near[0].append(forward(0, opposite, 3))
+    far[3].wait_recv()
     near[1].append(forward(1, left_chip, 1))
-    far[3].wait_recv()
+    far[4].wait_recv()
     rows = w_rows(w2, right)
     far.append(to_scene(rows, rows, w_s.at[1, 2], w_r.at[1, 2], left_chip))
     near[1].append(forward(1, right, 2))
-    opposite = (s + 4) % SC
-    far[4].wait_recv()
-    near[0].append(forward(0, opposite, 3))
-
-    m_t = jnp.concatenate([masked[t].astype(F32).T.astype(BF) for t in range(2)], axis=1)
-    for name in names[3:]:
-        loads[name].wait()
-    far[5].wait_recv()
-    near[1].append(forward(1, opposite, 3))
     await_all(recv2.at[pl.ds(0, REG - 1)], a2a_r.at[2])
 
     came = recv2[...].astype(F32)
@@ -286,6 +301,8 @@
                     part = part + inner[i * LEFT:(i + 1) * LEFT]
                 left_x[t * LEFT:(t + 1) * LEFT, tap * C:(tap + 1) * C] = part.astype(BF)
 
+    far[5].wait_recv()
+    near[1].append(forward(1, opposite, 3))
     own[0].wait()
     for copy in near[0]:
         copy.wait_recv()
@@ -402,7 +419,7 @@
         for j in range(3):
             tap = 3 * i + j
             seen = jnp.concatenate([hidden_rows(t, i)[:, j * C:(j + 1) * C] for t in range(2)], axis=0)
-            g_f[tap * C:(tap + 1) * C, :] = dot(m_t, seen).T
+            g_f[tap * C:(tap + 1) * C, :] = dot_l(seen, masked[...].reshape(512, C))
     blocks(1)
     y_first(1)
 
@@ -418,8 +435,6 @@
 
     up, down = slice(0, 256), slice(16, 272)
     for t in range(2):
-        if t == 1:
-            y_second(1)
         m0 = jnp.concatenate([masked[t], dot(table["below"][...], halo[t]).astype(BF)], axis=0)
         m1 = (dot(table["back"][...], masked[t]) + dot(table["beside"][...], halo[t])).astype(BF)
         spread = (
@@ -431,7 +446,9 @@
         )
         for n in range(4):
             group = 4 * t + n
-            grad_t[:, group * 256:(group + 1) * 256] = (spread[n] * slopes[group]).T.astype(BF)
+            d_pre[group * 256:(group + 1) * 256, :] = (spread[n] * slopes[group]).astype(BF)
+
+    y_second(1)
 
     def own_rows(t, par, i, cp, j):
         row = (2 if par == 0 else 1) + i
@@ -439,17 +456,16 @@
         return x4[t, row // 2:row // 2 + 16, row % 2, :, lanes:lanes + C].reshape(256, C)
 
     for i in range(3):
-        if i == 2:
-            z_second_left = z_first(1)
         for j in range(3):
             tap = 3 * i + j
             seen = jnp.concatenate(
                 [own_rows(t, par, i, cp, j) for t in range(2) for par in range(2) for cp in range(2)], axis=0)
-            g_f[tap * C:(tap + 1) * C, :] = dot(grad_t[...], seen).T
+            g_f[tap * C:(tap + 1) * C, :] = dot_l(seen, d_pre[...])
     blocks(0)
     y_first(0)
+    z_left = z_first(1)
     y_second(0)
-    total_second = z_second(1, *z_second_left)
+    total_second = z_second(1, *z_left)
     total_first = z_second(0, *z_first(0))
 
     squares = jnp.sum(total_first * total_first + total_second * total_second, axis=0, keepdims=True)
@@ -501,10 +517,12 @@
         level_kernel,
         name="level",
         out_shape=(jax.ShapeDtypeStruct((2, 16, 16, C), BF), jax.ShapeDtypeStruct((2, 32, OWN_ROWS), F32)),
-        in_specs=[vmem] * 4 + [anywhere] * (2 + len(tables)),
+        in_specs=[anywhere] * (6 + len(tables)),
         out_specs=(vmem, vmem),
         scratch_shapes=[pltpu.VMEM(t.shape, BF) for t in tables] + [
-            dma((len(tables),)),
+            pltpu.VMEM((1, 2), jnp.int32), pltpu.VMEM((1, 2), jnp.int32),
+            pltpu.VMEM((2, 32, 32, C), BF), pltpu.VMEM((2, 16, 16, C), BF),
+            dma((4,)), dma((len(tables),)),
             pltpu.VMEM((2, 1, 128), F32), pltpu.VMEM((2 * REG, 1, 128), F32),
             pltpu.VMEM((REG, 16, C), BF), pltpu.VMEM((REG, 16, C), BF),
             pltpu.VMEM((REG, 16, C), BF), pltpu.VMEM((REG, 16, C), BF),
@@ -514,7 +532,7 @@
             pltpu.VMEM((2, 17, 16, 3 * C), BF), pltpu.VMEM((2, 16, 16, 3 * C), BF),
             pltpu.VMEM((2 * LEFT, ROWS), BF),
             pltpu.VMEM((8, 256, C), F32),
-            pltpu.VMEM((C, 2048), BF),
+            pltpu.VMEM((2048, C), BF),
             pltpu.VMEM((ROWS, C), F32),
             pltpu.VMEM((2, YN, ZN) + part, BF),
             pltpu.VMEM((2, ZN) + part, BF), pltpu.VMEM((2, ZN) + part, BF),

time: 81.4 us -> 77.9 us (0.957)
  Pallas kernels: 77.5 us -> 74 us
    pallas_call x1, Pallas kernels: 77.5 us -> 74 us  [level(): pl.pallas_call(level_kernel, name='level', out_shape=(jax.ShapeDtypeStruc...]
where the time goes in v3:
time: 77.9 us; the launch traced here: 77.7 us
  Pallas kernels  74 us (95%)
  local copies, waits for them, and re-layouts  3.02 us (4%)
    pallas_call x1, Pallas kernels, level(): pl.pallas_call(level_kernel, name='level', out_shape=(jax.ShapeDtypeStruc...  74 us
    unnamed x1, local copies, waits for them, and re-layouts  1.67 us

profile of v3, /device:TPU:1, one launch (start us, length us, event | category | flops | bytes accessed | tf_op | source)
XLA Modules:
  0.0 77.7 jit_solution(9691925400762816917)
XLA Ops:
  0.6 74.0 %level.1 = (bf16[2,16,16,256]{3,2,1,0:T(8,128)(2,1)}, f32[2,32,72]{2,1,0:T(8,128)}) custom-call(s32[1,2]{1,0:T(1,128)} %positions_hbm.1, s32[1,2]{1,0:T(1,128)} %clear_hbm.1, bf16[2,32,32,256]{3,2,1,0:T(8,128)(2,1)} %bitcast.11, bf16[2,16,16,256]{3,2,1,0:T(8,128)(2,1)} %bitcast.12, bf16[288,256]{1,0:T(8,128)(2,1)} %w1_here.1, bf16[288,256]{1,0:T(8,128)(2,1)} %w2_here.1, ...), custom_call_target="tpu_custom_call" | custom-call | tf_op jit(solution)/shard_map/level/pallas_call | solution.py:516
  74.6 1.3 %slice_bitcast_fusion = (f32[72,32]{0,1:T(8,128)}, f32[72,32]{0,1:T(8,128)}) fusion(f32[2,32,72]{2,1,0:T(8,128)} %get-tuple-element.6), kind=kLoop, calls=%fused_computation | loop fusion | bytes 36864 | tf_op jit(solution)/shard_map/transpose | solution.py:555
  76.0 1.7 %copy.22 = bf16[1,2,16,16,256]{4,3,2,1,0:T(8,128)(2,1)} copy(bf16[1,2,16,16,256]{4,3,2,1,0:T(8,128)(2,1)} %bitcast.13) | data formatting | bytes 524288

commit v4 on v3

--- a/solution.py
+++ b/solution.py
@@ -158,11 +158,17 @@
 
     barrier = pltpu.get_barrier_semaphore()
 
+    def far_first(o):
+        step, turn_y = o // YN, o % YN
+        dz = ZN // 2 + ((step + 1) // 2) * (1 - 2 * (step % 2))
+        dy = YN // 2 + ((turn_y + 1) // 2) * (1 - 2 * (turn_y % 2))
+        return ((z + dz) % ZN) * YN + (y + dy) % YN
+
     def greet(o, carry):
-        pl.semaphore_signal(barrier, inc=1, device_id={"region": (r + o) % REG}, device_id_type=MESH)
+        pl.semaphore_signal(barrier, inc=1, device_id={"region": far_first(o)}, device_id_type=MESH)
         return carry
 
-    lax.fori_loop(1, REG, greet, 0)
+    lax.fori_loop(0, REG - 1, greet, 0)
     for o in range(1, SC):
         pl.semaphore_signal(barrier, inc=1, device_id={"scene": (s + o) % SC}, device_id_type=MESH)
 
@@ -176,10 +182,7 @@
 
     def all_to_all(n, src, dst):
         def send(o, carry):
-            step, turn_y = o // YN, o % YN
-            dz = ZN // 2 + ((step + 1) // 2) * (1 - 2 * (step % 2))
-            dy = YN // 2 + ((turn_y + 1) // 2) * (1 - 2 * (turn_y % 2))
-            to = ((z + dz) % ZN) * YN + (y + dy) % YN
+            to = far_first(o)
             pltpu.make_async_remote_copy(
                 src_ref=src(to), dst_ref=dst(r), send_sem=a2a_s.at[n], recv_sem=a2a_r.at[n],
                 device_id={"region": to}, device_id_type=MESH).start()
@@ -229,9 +232,12 @@
         rim = dot(table["rim"][...], tiles[t].reshape(1024, C)) + dot(table["rim_grad"][...], masked[t])
         own_rim[t] = rim.astype(BF)
         rims.append(rim.reshape(REG, 8, C))
-    send1[...] = jnp.concatenate(rims, axis=1).astype(BF)
-    all_to_all(1, lambda to: send1.at[to], lambda me: recv1.at[me])
-    recv1[r] = send1[r]
+    rims = jnp.concatenate(rims, axis=1).astype(BF)
+    for half in range(2):
+        send1[half] = rims[:, :, half * 128:(half + 1) * 128]
+        all_to_all(1 + half, lambda to: send1.at[half, to], lambda me: recv1.at[half, me])
+    for half in range(2):
+        recv1[half, r] = send1[half, r]
     for t in range(2):
         pos_buf[2 * r + t] = pos_send[t]
 
@@ -258,10 +264,12 @@
     send_weights(1)
     await_all(pos_buf.at[pl.ds(0, 2 * REG - 2)], a2a_r.at[0])
     route = route_rows(jnp.broadcast_to(pos_buf[...], (64, 8, 128)).reshape(512, 128), r)
-    await_all(recv1.at[pl.ds(0, REG - 1)], a2a_r.at[1])
-    send2[...] = dot(route, recv1[...].reshape(512, C)).astype(BF).reshape(REG, 16, C)
-    all_to_all(2, lambda to: send2.at[to], lambda me: recv2.at[me])
-    recv2[r] = send2[r]
+    for half in range(2):
+        await_all(recv1.at[half, pl.ds(0, REG - 1)], a2a_r.at[1 + half])
+        send2[half] = dot(route, recv1[half].reshape(512, 128)).astype(BF).reshape(REG, 16, 128)
+        all_to_all(3 + half, lambda to: send2.at[half, to], lambda me: recv2.at[half, me])
+    for half in range(2):
+        recv2[half, r] = send2[half, r]
 
     for name in names[3:]:
         loads[name].wait()
@@ -273,11 +281,11 @@
     rows = w_rows(w2, right)
     far.append(to_scene(rows, rows, w_s.at[1, 2], w_r.at[1, 2], left_chip))
     near[1].append(forward(1, right, 2))
-    await_all(recv2.at[pl.ds(0, REG - 1)], a2a_r.at[2])
-
-    came = recv2[...].astype(F32)
-    for t in range(2):
-        halo[t] = came[:, 8 * t:8 * t + 8].reshape(256, C).astype(BF)
+    for half in range(2):
+        await_all(recv2.at[half, pl.ds(0, REG - 1)], a2a_r.at[3 + half])
+        came = recv2[half].astype(F32)
+        for t in range(2):
+            halo[t, :, half * 128:(half + 1) * 128] = came[:, 8 * t:8 * t + 8].reshape(256, 128).astype(BF)
     for t in range(2):
         for c in range(4):
             chunk = tiles[t, 8 * c:8 * c + 8].reshape(256, C)
@@ -301,8 +309,6 @@
                     part = part + inner[i * LEFT:(i + 1) * LEFT]
                 left_x[t * LEFT:(t + 1) * LEFT, tap * C:(tap + 1) * C] = part.astype(BF)
 
-    far[5].wait_recv()
-    near[1].append(forward(1, opposite, 3))
     own[0].wait()
     for copy in near[0]:
         copy.wait_recv()
@@ -325,6 +331,9 @@
         return x4[t, row // 2:row // 2 + n, row % 2, :, cp * C:cp * C + 768].reshape(n * 16, 768)
 
     for t in range(2):
+        if t == 1:
+            far[5].wait_recv()
+            near[1].append(forward(1, opposite, 3))
         for par in range(2):
             store = h_odd if par == 0 else h_even
             n = 17 - par
@@ -470,7 +479,7 @@
 
     squares = jnp.sum(total_first * total_first + total_second * total_second, axis=0, keepdims=True)
     n_send[0] = squares
-    all_to_all(3, lambda to: n_send.at[0], lambda me: n_buf.at[me])
+    all_to_all(5, lambda to: n_send.at[0], lambda me: n_buf.at[me])
     n_buf[r] = squares
     for n, total in enumerate((total_first, total_second)):
         turned = jnp.concatenate([total[:OWN_ROWS].T, total[OWN_ROWS:].T], axis=0)
@@ -479,7 +488,7 @@
     for o in range(1, SC):
         to = (s + o) % SC
         x_copies.append(to_scene(x_send.at[to], x_buf.at[o - 1], xs.at[o - 1], xr.at[o - 1], to))
-    await_all(n_buf.at[pl.ds(0, REG - 1)], a2a_r.at[3])
+    await_all(n_buf.at[pl.ds(0, REG - 1)], a2a_r.at[5])
     sum_sq = jnp.sum(n_buf[...].reshape(REG, 128), keepdims=True)
     factor = (3.0 * C * math.sqrt(2.0) / SC) / (jnp.sqrt(sum_sq) + 0.01)
     c_send[0] = jnp.broadcast_to(factor, (1, 128))
@@ -497,9 +506,10 @@
     for copy in far + near[0] + near[1] + sent + x_copies + c_copies:
         copy.wait_send()
     await_all(pos_buf.at[pl.ds(0, 2 * REG - 2)], a2a_s.at[0])
-    await_all(send1.at[pl.ds(0, REG - 1)], a2a_s.at[1])
-    await_all(send2.at[pl.ds(0, REG - 1)], a2a_s.at[2])
-    await_all(n_buf.at[pl.ds(0, REG - 1)], a2a_s.at[3])
+    for half in range(2):
+        await_all(send1.at[half, pl.ds(0, REG - 1)], a2a_s.at[1 + half])
+        await_all(send2.at[half, pl.ds(0, REG - 1)], a2a_s.at[3 + half])
+    await_all(n_buf.at[pl.ds(0, REG - 1)], a2a_s.at[5])
 
 
 NAMES = ("rim", "rim_grad", "body", "sides", "edges", "left", "first_col", "shift", "from_left",
@@ -524,8 +534,8 @@
             pltpu.VMEM((2, 32, 32, C), BF), pltpu.VMEM((2, 16, 16, C), BF),
             dma((4,)), dma((len(tables),)),
             pltpu.VMEM((2, 1, 128), F32), pltpu.VMEM((2 * REG, 1, 128), F32),
-            pltpu.VMEM((REG, 16, C), BF), pltpu.VMEM((REG, 16, C), BF),
-            pltpu.VMEM((REG, 16, C), BF), pltpu.VMEM((REG, 16, C), BF),
+            pltpu.VMEM((2, REG, 16, 128), BF), pltpu.VMEM((2, REG, 16, 128), BF),
+            pltpu.VMEM((2, REG, 16, 128), BF), pltpu.VMEM((2, REG, 16, 128), BF),
             pltpu.VMEM((2, 256, C), BF), pltpu.VMEM((2, 256, C), BF), pltpu.VMEM((2, 256, C), BF),
             pltpu.VMEM((ROWS, C), BF), pltpu.VMEM((ROWS, C), BF),
             pltpu.VMEM((2, 18, 2, 16, 4 * C), BF),
@@ -541,7 +551,7 @@
             pltpu.VMEM((1, 1, 128), F32), pltpu.VMEM((REG, 1, 128), F32),
             pltpu.VMEM((SC, 2, 32, OWN_ROWS), F32), pltpu.VMEM((SC - 1, 2, 32, OWN_ROWS), F32),
             pltpu.VMEM((1, 1, 128), F32), pltpu.VMEM((SC - 1, 1, 128), F32),
-            dma((4,)), dma((4,)), dma((2, 3)), dma((2, 3)), dma((2, 4)), dma((2, 4)),
+            dma((6,)), dma((6,)), dma((2, 3)), dma((2, 3)), dma((2, 4)), dma((2, 4)),
             dma((3, 2, ZN)), dma((3, 2, ZN)), dma((2, ZN - 1)), dma((2, ZN - 1)),
             dma((SC - 1,)), dma((SC - 1,)), dma((SC - 1,)), dma((SC - 1,)), dma((2,)),
         ],

time: 77.9 us -> 75.9 us (0.974)
  Pallas kernels: 74 us -> 72 us
    pallas_call x1, Pallas kernels: 74 us -> 72 us  [level(): pl.pallas_call(level_kernel, name='level', out_shape=(jax.ShapeDtypeStruc...]
where the time goes in v4:
time: 75.9 us; the launch traced here: 75.6 us
  Pallas kernels  72 us (95%)
  local copies, waits for them, and re-layouts  3.02 us (4%)
    pallas_call x1, Pallas kernels, level(): pl.pallas_call(level_kernel, name='level', out_shape=(jax.ShapeDtypeStruc...  72 us
    unnamed x1, local copies, waits for them, and re-layouts  1.67 us

profile of v4, /device:TPU:1, one launch (start us, length us, event | category | flops | bytes accessed | tf_op | source)
XLA Modules:
  0.0 75.6 jit_solution(4067566549259065074)
XLA Ops:
  0.6 72.0 %level.1 = (bf16[2,16,16,256]{3,2,1,0:T(8,128)(2,1)}, f32[2,32,72]{2,1,0:T(8,128)}) custom-call(s32[1,2]{1,0:T(1,128)} %positions_hbm.1, s32[1,2]{1,0:T(1,128)} %clear_hbm.1, bf16[2,32,32,256]{3,2,1,0:T(8,128)(2,1)} %bitcast.11, bf16[2,16,16,256]{3,2,1,0:T(8,128)(2,1)} %bitcast.12, bf16[288,256]{1,0:T(8,128)(2,1)} %w1_here.1, bf16[288,256]{1,0:T(8,128)(2,1)} %w2_here.1, ...), custom_call_target="tpu_custom_call" | custom-call | tf_op jit(solution)/shard_map/level/pallas_call | solution.py:526
  72.6 1.3 %slice_bitcast_fusion = (f32[72,32]{0,1:T(8,128)}, f32[72,32]{0,1:T(8,128)}) fusion(f32[2,32,72]{2,1,0:T(8,128)} %get-tuple-element.6), kind=kLoop, calls=%fused_computation | loop fusion | bytes 36864 | tf_op jit(solution)/shard_map/transpose | solution.py:565
  74.0 1.7 %copy.22 = bf16[1,2,16,16,256]{4,3,2,1,0:T(8,128)(2,1)} copy(bf16[1,2,16,16,256]{4,3,2,1,0:T(8,128)(2,1)} %bitcast.13) | data formatting | bytes 524288

commit v5 on v4

--- a/solution.py
+++ b/solution.py
@@ -128,19 +128,20 @@
     return jnp.where(same, dot_t(wants, has), 0.0).astype(BF)
 
 
+Z_PART = 32
 Z_ORDER = (4, 3, 5, 2, 6, 1, 7, 0)
 
 
 def level_kernel(positions_hbm, clear_hbm, tiles_hbm, cotangent_hbm, w1_here, w2_here, *refs):
     names = list(TABLES)
     table_hbm = dict(zip(names, refs[:len(names)]))
-    feat, out = refs[len(names):len(names) + 2]
+    feat_hbm, out = refs[len(names):len(names) + 2]
     refs = refs[len(names) + 2:]
     table = dict(zip(names, refs[:len(names)]))
-    (positions, clear, tiles, cotangent, in_sem, table_sem, pos_send, pos_buf, send1, recv1, send2, recv2, masked, own_rim, halo, w1, w2,
+    (positions, clear, tiles, cotangent, feat, feat_sem, in_sem, table_sem, pos_send, pos_buf, send1, recv1, send2, recv2, masked, own_rim, halo, w1, w2,
      x4, h_odd, h_even, left_x, slopes, d_pre, g_f, g, f_buf, o_buf, s_buf, s_send, z_send, z_buf,
-     n_send, n_buf, x_send, x_buf, c_send, c_buf,
-     a2a_s, a2a_r, w_s, w_r, v_s, v_r, y_s, y_r, zs, zr, xs, xr, cs, cr, own_sem) = refs[len(names):]
+     other_z, other_sum, other_send, other_y, n_send, n_buf, x_send, x_buf, c_send, c_buf,
+     a2a_s, a2a_r, w_s, w_r, v_s, v_r, y_s, y_r, zs, zr, o_s, o_r, xs, xr, cs, cr, own_sem) = refs[len(names):]
 
     s = lax.axis_index("scene")
     r = lax.axis_index("region")
@@ -378,6 +379,7 @@
 
     sent = []
     y_copies = {}
+    held = (144, 144 - Z_PART)
 
     def turn(oz):
         return 1 if oz % 2 == 0 else YN - 1
@@ -390,7 +392,7 @@
                 who = (y + d) % YN if kind == 0 else block
                 buf = f_buf if kind == 0 else o_buf
                 y_copies[n, kind, oz] = to_region(
-                    g.at[n, block, (z + oz) % ZN], buf.at[n, oz],
+                    g.at[n, block, (z + oz) % ZN, pl.ds(0, held[n])], buf.at[n, oz, pl.ds(0, held[n])],
                     y_s.at[kind, n, oz], y_r.at[kind, n, oz], z * YN + who)
                 sent.append(y_copies[n, kind, oz])
 
@@ -398,10 +400,10 @@
         for oz in Z_ORDER:
             who = (y + turn(oz)) % YN
             y_copies[n, 0, oz].wait_recv()
-            summed = g[n, who, (z + oz) % ZN].astype(F32) + f_buf[n, oz].astype(F32)
-            s_send[n, oz] = summed.astype(BF)
+            summed = g[n, who, (z + oz) % ZN, :held[n]].astype(F32) + f_buf[n, oz, :held[n]].astype(F32)
+            s_send[n, oz, :held[n]] = summed.astype(BF)
             y_copies[n, 2, oz] = to_region(
-                s_send.at[n, oz], s_buf.at[n, oz], y_s.at[2, n, oz], y_r.at[2, n, oz], z * YN + who)
+                s_send.at[n, oz, pl.ds(0, held[n])], s_buf.at[n, oz, pl.ds(0, held[n])], y_s.at[2, n, oz], y_r.at[2, n, oz], z * YN + who)
             sent.append(y_copies[n, 2, oz])
 
     def z_first(n):
@@ -409,11 +411,12 @@
         for oz in Z_ORDER:
             y_copies[n, 1, oz].wait_recv()
             y_copies[n, 2, oz].wait_recv()
-            total = (g[n, y, (z + oz) % ZN].astype(F32) + o_buf[n, oz].astype(F32)) + s_buf[n, oz].astype(F32)
+            total = g[n, y, (z + oz) % ZN, :held[n]].astype(F32) + o_buf[n, oz, :held[n]].astype(F32)
+            total = total + s_buf[n, oz, :held[n]].astype(F32)
             if oz:
-                z_send[n, oz - 1] = total.astype(BF)
+                z_send[n, oz - 1, :held[n]] = total.astype(BF)
                 copies.append(to_region(
-                    z_send.at[n, oz - 1], z_buf.at[n, oz - 1], zs.at[n, oz - 1], zr.at[n, oz - 1],
+                    z_send.at[n, oz - 1, pl.ds(0, held[n])], z_buf.at[n, oz - 1, pl.ds(0, held[n])], zs.at[n, oz - 1], zr.at[n, oz - 1],
                     ((z + oz) % ZN) * YN + y))
         sent.extend(copies)
         return total, copies
@@ -421,7 +424,34 @@
     def z_second(n, total, copies):
         for at, copy in enumerate(copies):
             copy.wait_recv()
-            total = total + z_buf[n, Z_ORDER[at] - 1].astype(F32)
+            total = total + z_buf[n, Z_ORDER[at] - 1, :held[n]].astype(F32)
+        return total
+
+    def other_first():
+        copies = [to_region(
+            g.at[1, :, (z + oz) % ZN, pl.ds(held[1], Z_PART)], other_z.at[oz - 1],
+            o_s.at[oz - 1], o_r.at[oz - 1], ((z + oz) % ZN) * YN + y) for oz in Z_ORDER[:-1]]
+        sent.extend(copies)
+        return copies
+
+    def other_second(copies):
+        total = g[1, :, z, held[1]:].astype(F32)
+        for at, copy in enumerate(copies):
+            copy.wait_recv()
+            total = total + other_z[Z_ORDER[at] - 1].astype(F32)
+        other_sum[...] = total
+        other_send[...] = total.astype(BF)
+        copies = [to_region(
+            other_send.at[(y + o) % YN], other_y.at[o - 1], o_s.at[ZN + o - 2], o_r.at[ZN + o - 2],
+            z * YN + (y + o) % YN) for o in range(1, YN)]
+        sent.extend(copies)
+        return copies
+
+    def other_third(copies):
+        total = other_sum[y]
+        for at, copy in enumerate(copies):
+            copy.wait_recv()
+            total = total + other_y[at].astype(F32)
         return total
 
     for i in range(3):
@@ -431,6 +461,7 @@
             g_f[tap * C:(tap + 1) * C, :] = dot_l(seen, masked[...].reshape(512, C))
     blocks(1)
     y_first(1)
+    other = other_first()
 
     own[1].wait()
     for copy in near[1]:
@@ -438,6 +469,8 @@
     for t in range(2):
         patch = jnp.concatenate([hidden_rows(t, i) for i in range(3)], axis=1)
         feat[t] = dot(patch, w2[...]).astype(BF).reshape(16, 16, C)
+    feat_copy = pltpu.make_async_copy(feat, feat_hbm, feat_sem)
+    feat_copy.start()
 
     def second(tap):
         return w2[tap * C:(tap + 1) * C, :]
@@ -472,9 +505,10 @@
             g_f[tap * C:(tap + 1) * C, :] = dot_l(seen, d_pre[...])
     blocks(0)
     y_first(0)
+    other = other_second(other)
     z_left = z_first(1)
     y_second(0)
-    total_second = z_second(1, *z_left)
+    total_second = jnp.concatenate([z_second(1, *z_left), other_third(other)], axis=0)
     total_first = z_second(0, *z_first(0))
 
     squares = jnp.sum(total_first * total_first + total_second * total_second, axis=0, keepdims=True)
@@ -502,6 +536,7 @@
         c_copies[o - 1].wait_recv()
         result = result + x_buf[o - 1] * c_buf[o - 1][:, :1].reshape(1, 1, 1)
     out[...] = result
+    feat_copy.wait()
 
     for copy in far + near[0] + near[1] + sent + x_copies + c_copies:
         copy.wait_send()
@@ -528,11 +563,11 @@
         name="level",
         out_shape=(jax.ShapeDtypeStruct((2, 16, 16, C), BF), jax.ShapeDtypeStruct((2, 32, OWN_ROWS), F32)),
         in_specs=[anywhere] * (6 + len(tables)),
-        out_specs=(vmem, vmem),
+        out_specs=(anywhere, vmem),
         scratch_shapes=[pltpu.VMEM(t.shape, BF) for t in tables] + [
             pltpu.VMEM((1, 2), jnp.int32), pltpu.VMEM((1, 2), jnp.int32),
             pltpu.VMEM((2, 32, 32, C), BF), pltpu.VMEM((2, 16, 16, C), BF),
-            dma((4,)), dma((len(tables),)),
+            pltpu.VMEM((2, 16, 16, C), BF), dma, dma((4,)), dma((len(tables),)),
             pltpu.VMEM((2, 1, 128), F32), pltpu.VMEM((2 * REG, 1, 128), F32),
             pltpu.VMEM((2, REG, 16, 128), BF), pltpu.VMEM((2, REG, 16, 128), BF),
             pltpu.VMEM((2, REG, 16, 128), BF), pltpu.VMEM((2, REG, 16, 128), BF),
@@ -548,11 +583,13 @@
             pltpu.VMEM((2, ZN) + part, BF), pltpu.VMEM((2, ZN) + part, BF),
             pltpu.VMEM((2, ZN) + part, BF), pltpu.VMEM((2, ZN) + part, BF),
             pltpu.VMEM((2, ZN - 1) + part, BF), pltpu.VMEM((2, ZN - 1) + part, BF),
+            pltpu.VMEM((ZN - 1, YN, Z_PART, 128), BF), pltpu.VMEM((YN, Z_PART, 128), F32),
+            pltpu.VMEM((YN, Z_PART, 128), BF), pltpu.VMEM((YN - 1, Z_PART, 128), BF),
             pltpu.VMEM((1, 1, 128), F32), pltpu.VMEM((REG, 1, 128), F32),
             pltpu.VMEM((SC, 2, 32, OWN_ROWS), F32), pltpu.VMEM((SC - 1, 2, 32, OWN_ROWS), F32),
             pltpu.VMEM((1, 1, 128), F32), pltpu.VMEM((SC - 1, 1, 128), F32),
             dma((6,)), dma((6,)), dma((2, 3)), dma((2, 3)), dma((2, 4)), dma((2, 4)),
-            dma((3, 2, ZN)), dma((3, 2, ZN)), dma((2, ZN - 1)), dma((2, ZN - 1)),
+            dma((3, 2, ZN)), dma((3, 2, ZN)), dma((2, ZN - 1)), dma((2, ZN - 1)), dma((ZN + YN - 2,)), dma((ZN + YN - 2,)),
             dma((SC - 1,)), dma((SC - 1,)), dma((SC - 1,)), dma((SC - 1,)), dma((2,)),
         ],
         compiler_params=pltpu.CompilerParams(
@@ -560,9 +597,28 @@
     )(positions, clear, tiles, cotangent, w1, w2, *[jnp.asarray(t) for t in tables])
 
 
+def finish_kernel(feat_in, out_in, feat, first, second):
+    feat[...] = feat_in[...]
+    first[...] = out_in[0]
+    second[...] = out_in[1]
+
+
+def finish(feat, out):
+    vmem = pl.BlockSpec(memory_space=pltpu.VMEM)
+    share = jax.ShapeDtypeStruct((32, OWN_ROWS), F32)
+    return pl.pallas_call(
+        finish_kernel,
+        name="finish",
+        out_shape=(jax.ShapeDtypeStruct(feat.shape, BF), share, share),
+        in_specs=[vmem, vmem],
+        out_specs=(vmem, vmem, vmem),
+    )(feat, out)
+
+
 def local(tiles, cotangent, positions, clear, w_first, w_second):
     feat, out = level(positions, clear, tiles[0], cotangent[0], w_first, w_second)
-    return feat[None], out[0].T, out[1].T
+    feat, first, second = finish(feat, out)
+    return feat[None], first.T, second.T
 
 
 def solution(mesh):

time: 75.9 us -> 73.1 us (0.963)
  local copies, waits for them, and re-layouts: 3.02 us -> 0 us
    pallas_call x0 -> x1, Pallas kernels: none -> 1.68 us  [finish(): pl.pallas_call(finish_kernel, name='finish', out_shape=(jax.ShapeDtypeStr...]
    unnamed x1 -> x0, local copies, waits for them, and re-layouts: 1.67 us -> none
    transpose x1 -> x0, local copies, waits for them, and re-layouts: 1.35 us -> none  [local(): return (feat[None], out[0].T, out[1].T)]
    pallas_call x1, Pallas kernels: 72 us -> 70.7 us  [level(): pl.pallas_call(level_kernel, name='level', out_shape=(jax.ShapeDtypeStruc...]
where the time goes in v5:
time: 73.1 us; the launch traced here: 73 us
  Pallas kernels  72.4 us (99%)
    pallas_call x1, Pallas kernels, level(): pl.pallas_call(level_kernel, name='level', out_shape=(jax.ShapeDtypeStruc...  70.7 us
    pallas_call x1, Pallas kernels, finish(): pl.pallas_call(finish_kernel, name='finish', out_shape=(jax.ShapeDtypeStr...  1.68 us

profile of v5, /device:TPU:1, one launch (start us, length us, event | category | flops | bytes accessed | tf_op | source)
XLA Modules:
  0.0 73.0 jit_solution(2091875146768865097)
XLA Ops:
  0.6 70.7 %level.1 = (bf16[2,16,16,256]{3,2,1,0:T(8,128)(2,1)}, f32[2,32,72]{2,1,0:T(8,128)}) custom-call(s32[1,2]{1,0:T(1,128)} %positions_hbm.1, s32[1,2]{1,0:T(1,128)} %clear_hbm.1, bf16[2,32,32,256]{3,2,1,0:T(8,128)(2,1)} %bitcast.5, bf16[2,16,16,256]{3,2,1,0:T(8,128)(2,1)} %bitcast.6, bf16[288,256]{1,0:T(8,128)(2,1)} %w1_here.1, bf16[288,256]{1,0:T(8,128)(2,1)} %w2_here.1, ...), custom_call_target="tpu_custom_call" | custom-call | tf_op jit(solution)/shard_map/level/pallas_call | solution.py:561
  71.3 1.7 %finish.1 = (bf16[2,16,16,256]{3,2,1,0:T(8,128)(2,1)}, f32[32,72]{1,0:T(8,128)}, f32[32,72]{1,0:T(8,128)}) custom-call(bf16[2,16,16,256]{3,2,1,0:T(8,128)(2,1)} %get-tuple-element.8.feat_in, f32[2,32,72]{2,1,0:T(8,128)} %get-tuple-element.9.out_in), custom_call_target="tpu_custom_call" | custom-call | tf_op jit(solution)/shard_map/finish/pallas_call | solution.py:609

commit v6 on v5

--- a/solution.py
+++ b/solution.py
@@ -148,6 +148,22 @@
     z, y = r // YN, r % YN
     sib = s + 1 - 2 * (s % 2)
 
+    barrier = pltpu.get_barrier_semaphore()
+
+    def far_first(o):
+        step, turn_y = o // YN, o % YN
+        dz = ZN // 2 + ((step + 1) // 2) * (1 - 2 * (step % 2))
+        dy = YN // 2 + ((turn_y + 1) // 2) * (1 - 2 * (turn_y % 2))
+        return ((z + dz) % ZN) * YN + (y + dy) % YN
+
+    def greet(o, carry):
+        pl.semaphore_signal(barrier, inc=1, device_id={"region": far_first(o)}, device_id_type=MESH)
+        return carry
+
+    lax.fori_loop(0, REG - 1, greet, 0)
+    for o in range(1, SC):
+        pl.semaphore_signal(barrier, inc=1, device_id={"scene": (s + o) % SC}, device_id_type=MESH)
+
     arrays = [pltpu.make_async_copy(src, dst, in_sem.at[n]) for n, (src, dst) in enumerate((
         (positions_hbm, positions), (clear_hbm, clear), (tiles_hbm, tiles), (cotangent_hbm, cotangent)))]
     for copy in arrays:
@@ -156,22 +172,6 @@
              for n, name in enumerate(names)}
     for name in names:
         loads[name].start()
-
-    barrier = pltpu.get_barrier_semaphore()
-
-    def far_first(o):
-        step, turn_y = o // YN, o % YN
-        dz = ZN // 2 + ((step + 1) // 2) * (1 - 2 * (step % 2))
-        dy = YN // 2 + ((turn_y + 1) // 2) * (1 - 2 * (turn_y % 2))
-        return ((z + dz) % ZN) * YN + (y + dy) % YN
-
-    def greet(o, carry):
-        pl.semaphore_signal(barrier, inc=1, device_id={"region": far_first(o)}, device_id_type=MESH)
-        return carry
-
-    lax.fori_loop(0, REG - 1, greet, 0)
-    for o in range(1, SC):
-        pl.semaphore_signal(barrier, inc=1, device_id={"scene": (s + o) % SC}, device_id_type=MESH)
 
     def w_rows(ref, who):
         return ref.at[pl.ds(pl.multiple_of(who * WROWS, 32), WROWS)]
@@ -509,15 +509,20 @@
     z_left = z_first(1)
     y_second(0)
     total_second = jnp.concatenate([z_second(1, *z_left), other_third(other)], axis=0)
-    total_first = z_second(0, *z_first(0))
-
-    squares = jnp.sum(total_first * total_first + total_second * total_second, axis=0, keepdims=True)
+
+    def share(n, total):
+        both = jnp.concatenate([total[:OWN_ROWS].T, total[OWN_ROWS:].T], axis=0)
+        x_send[:, n] = both.reshape(SC, 32, OWN_ROWS)
+
+    z_left = z_first(0)
+    share(1, total_second)
+    squares = jnp.sum(total_second * total_second, axis=0, keepdims=True)
+    total_first = z_second(0, *z_left)
+    squares = squares + jnp.sum(total_first * total_first, axis=0, keepdims=True)
     n_send[0] = squares
     all_to_all(5, lambda to: n_send.at[0], lambda me: n_buf.at[me])
     n_buf[r] = squares
-    for n, total in enumerate((total_first, total_second)):
-        turned = jnp.concatenate([total[:OWN_ROWS].T, total[OWN_ROWS:].T], axis=0)
-        x_send[:, n] = turned.reshape(SC, 32, OWN_ROWS)
+    share(0, total_first)
     x_copies = []
     for o in range(1, SC):
         to = (s + o) % SC

time: 73.1 us -> 73.1 us (level)
  no operation moved by 1% of the time
where the time goes in v6:
time: 73.1 us; the launch traced here: 73 us
  Pallas kernels  72.3 us (99%)
    pallas_call x1, Pallas kernels, level(): pl.pallas_call(level_kernel, name='level', out_shape=(jax.ShapeDtypeStruc...  70.7 us
    pallas_call x1, Pallas kernels, finish(): pl.pallas_call(finish_kernel, name='finish', out_shape=(jax.ShapeDtypeStr...  1.68 us

profile of v6, /device:TPU:1, one launch (start us, length us, event | category | flops | bytes accessed | tf_op | source)
XLA Modules:
  0.0 73.0 jit_solution(10859728155308719859)
XLA Ops:
  0.6 70.7 %level.1 = (bf16[2,16,16,256]{3,2,1,0:T(8,128)(2,1)}, f32[2,32,72]{2,1,0:T(8,128)}) custom-call(s32[1,2]{1,0:T(1,128)} %positions_hbm.1, s32[1,2]{1,0:T(1,128)} %clear_hbm.1, bf16[2,32,32,256]{3,2,1,0:T(8,128)(2,1)} %bitcast.5, bf16[2,16,16,256]{3,2,1,0:T(8,128)(2,1)} %bitcast.6, bf16[288,256]{1,0:T(8,128)(2,1)} %w1_here.1, bf16[288,256]{1,0:T(8,128)(2,1)} %w2_here.1, ...), custom_call_target="tpu_custom_call" | custom-call | tf_op jit(solution)/shard_map/level/pallas_call | solution.py:566
  71.3 1.7 %finish.1 = (bf16[2,16,16,256]{3,2,1,0:T(8,128)(2,1)}, f32[32,72]{1,0:T(8,128)}, f32[32,72]{1,0:T(8,128)}) custom-call(bf16[2,16,16,256]{3,2,1,0:T(8,128)(2,1)} %get-tuple-element.8.feat_in, f32[2,32,72]{2,1,0:T(8,128)} %get-tuple-element.9.out_in), custom_call_target="tpu_custom_call" | custom-call | tf_op jit(solution)/shard_map/finish/pallas_call | solution.py:614

commit v7 on v6

--- a/solution.py
+++ b/solution.py
@@ -490,14 +490,14 @@
             group = 4 * t + n
             d_pre[group * 256:(group + 1) * 256, :] = (spread[n] * slopes[group]).astype(BF)
 
-    y_second(1)
-
     def own_rows(t, par, i, cp, j):
         row = (2 if par == 0 else 1) + i
         lanes = (cp + j) * C
         return x4[t, row // 2:row // 2 + 16, row % 2, :, lanes:lanes + C].reshape(256, C)
 
     for i in range(3):
+        if i == 2:
+            y_second(1)
         for j in range(3):
             tap = 3 * i + j
             seen = jnp.concatenate(

time: 73.1 us -> 72.9 us (level)
  no operation moved by 1% of the time
where the time goes in v7:
time: 72.9 us; the launch traced here: 72.8 us
  Pallas kernels  72.2 us (99%)
    pallas_call x1, Pallas kernels, level(): pl.pallas_call(level_kernel, name='level', out_shape=(jax.ShapeDtypeStruc...  70.5 us
    pallas_call x1, Pallas kernels, finish(): pl.pallas_call(finish_kernel, name='finish', out_shape=(jax.ShapeDtypeStr...  1.68 us

profile of v7, /device:TPU:1, one launch (start us, length us, event | category | flops | bytes accessed | tf_op | source)
XLA Modules:
  0.0 72.8 jit_solution(13990669376366108539)
XLA Ops:
  0.6 70.5 %level.1 = (bf16[2,16,16,256]{3,2,1,0:T(8,128)(2,1)}, f32[2,32,72]{2,1,0:T(8,128)}) custom-call(s32[1,2]{1,0:T(1,128)} %positions_hbm.1, s32[1,2]{1,0:T(1,128)} %clear_hbm.1, bf16[2,32,32,256]{3,2,1,0:T(8,128)(2,1)} %bitcast.5, bf16[2,16,16,256]{3,2,1,0:T(8,128)(2,1)} %bitcast.6, bf16[288,256]{1,0:T(8,128)(2,1)} %w1_here.1, bf16[288,256]{1,0:T(8,128)(2,1)} %w2_here.1, ...), custom_call_target="tpu_custom_call" | custom-call | tf_op jit(solution)/shard_map/level/pallas_call | solution.py:566
  71.1 1.7 %finish.1 = (bf16[2,16,16,256]{3,2,1,0:T(8,128)(2,1)}, f32[32,72]{1,0:T(8,128)}, f32[32,72]{1,0:T(8,128)}) custom-call(bf16[2,16,16,256]{3,2,1,0:T(8,128)(2,1)} %get-tuple-element.8.feat_in, f32[2,32,72]{2,1,0:T(8,128)} %get-tuple-element.9.out_in), custom_call_target="tpu_custom_call" | custom-call | tf_op jit(solution)/shard_map/finish/pallas_call | solution.py:614

commit v8 on v6

--- a/solution.py
+++ b/solution.py
@@ -128,7 +128,7 @@
     return jnp.where(same, dot_t(wants, has), 0.0).astype(BF)
 
 
-Z_PART = 32
+Z_PART = 16
 Z_ORDER = (4, 3, 5, 2, 6, 1, 7, 0)
 
 

time: 73.1 us -> 73.9 us (1.011)
  Pallas kernels: 72.3 us -> 73.2 us
    pallas_call x1, Pallas kernels: 70.7 us -> 71.5 us  [level(): pl.pallas_call(level_kernel, name='level', out_shape=(jax.ShapeDtypeStruc...]
where the time goes in v8:
time: 73.9 us; the launch traced here: 73.8 us
  Pallas kernels  73.2 us (99%)
    pallas_call x1, Pallas kernels, level(): pl.pallas_call(level_kernel, name='level', out_shape=(jax.ShapeDtypeStruc...  71.5 us
    pallas_call x1, Pallas kernels, finish(): pl.pallas_call(finish_kernel, name='finish', out_shape=(jax.ShapeDtypeStr...  1.68 us

profile of v8, /device:TPU:1, one launch (start us, length us, event | category | flops | bytes accessed | tf_op | source)
XLA Modules:
  0.0 73.8 jit_solution(1346345058774539351)
XLA Ops:
  0.6 71.5 %level.1 = (bf16[2,16,16,256]{3,2,1,0:T(8,128)(2,1)}, f32[2,32,72]{2,1,0:T(8,128)}) custom-call(s32[1,2]{1,0:T(1,128)} %positions_hbm.1, s32[1,2]{1,0:T(1,128)} %clear_hbm.1, bf16[2,32,32,256]{3,2,1,0:T(8,128)(2,1)} %bitcast.5, bf16[2,16,16,256]{3,2,1,0:T(8,128)(2,1)} %bitcast.6, bf16[288,256]{1,0:T(8,128)(2,1)} %w1_here.1, bf16[288,256]{1,0:T(8,128)(2,1)} %w2_here.1, ...), custom_call_target="tpu_custom_call" | custom-call | tf_op jit(solution)/shard_map/level/pallas_call | solution.py:566
  72.1 1.7 %finish.1 = (bf16[2,16,16,256]{3,2,1,0:T(8,128)(2,1)}, f32[32,72]{1,0:T(8,128)}, f32[32,72]{1,0:T(8,128)}) custom-call(bf16[2,16,16,256]{3,2,1,0:T(8,128)(2,1)} %get-tuple-element.8.feat_in, f32[2,32,72]{2,1,0:T(8,128)} %get-tuple-element.9.out_in), custom_call_target="tpu_custom_call" | custom-call | tf_op jit(solution)/shard_map/finish/pallas_call | solution.py:614
